TPU v7x, 128 devices: a whole 4x4x4 slice. The times are simulated.
128 devices in a mesh: src: 16 (over y_hi, z, core), rep: 8 (over y_lo, x).
Axes of the slice: x: 4, y: 4 (y_hi: 2, y_lo: 2; y = y_hi * 2 + y_lo), z: 4, core: 2. Of those that a mesh axis runs over, the one named last changes fastest.
Arguments:
- queries: bfloat16 [16384, 512], P(('src', 'rep')), may hold values from -6 to 6
- out_grad: bfloat16 [16384, 512], P(('src', 'rep')), may hold values from -48 to 48
- outputs: bfloat16 [16384, 512], P(('src', 'rep')), may hold values from -6 to 6
- log_norms: float32 [4, 16384], P(None, ('src', 'rep')), may hold values from 6 to 8
- src_keys: bfloat16 [16384, 512], P('src'), may hold values from -6 to 6
- src_values: bfloat16 [16384, 512], P('src'), may hold values from -6 to 6
- block_list: int32 [16, 8, 2, 96], P('src', 'rep'), may hold values from 0 to 15, as said below
- block_count: int32 [16, 8], P('src', 'rep'), may hold values from 1 to 96, as said below
- mask_bits: int32 [16, 8, 96, 8, 128], P('src', 'rep'), may hold values from 0 to 65535
Outputs:
- query_grad: bfloat16 [16384, 512], P(('src', 'rep'))
- key_grad: bfloat16 [16384, 512], P(('src', 'rep'))
- value_grad: bfloat16 [16384, 512], P(('src', 'rep'))
Inputs may be any that keep to these rules, and one draw needn't show every extreme that they name: `block_list`: row 0 holds destination blocks 0 to 15 of the group, row 1 source blocks 0 to 7 of the shard; the 96 pairs of one (s, r) are distinct. `block_count`: one source shard has 96 live entries in every group. `mask_bits`: bit b (counted from the lowest) of word w at column c is the edge from source row c to destination row 16 w + b of the block pair; bits for rows at or past 128, where there are any, are ignored.
All inputs are finite; a program needn't handle non-finite values.
Results may differ from a plain program's by a relative error of at most 0.0049.
Values may be sent and summed in bfloat16 or wider, within the bound.
A program may use at most 64 MiB of HBM per device.

v0:
```python
import jax
import jax.numpy as jnp
from jax import lax
from jax.sharding import PartitionSpec as P


def unpack_mask(packed):
    shifts = jnp.arange(16, dtype=jnp.int32)
    bit_values = jnp.bitwise_and(jnp.right_shift(packed[..., :, None, :], shifts[:, None]), 1)
    lead = packed.shape[:-2]
    bit_values = bit_values.reshape(lead + (packed.shape[-2] * 16, packed.shape[-1]))
    return bit_values


def shards(
    queries, out_grad, outputs, log_norms, src_keys, src_values, block_list, block_count, mask_bits
):
    head_count = log_norms.shape[0]
    features = queries.shape[1]
    head_dim = features // head_count
    block_len = mask_bits.shape[-1]
    score_scale = head_dim ** (-0.5)
    local_rows = queries.shape[0]
    products = out_grad.astype(jnp.float32) * outputs.astype(jnp.float32)
    row_delta = jnp.sum(products.reshape(local_rows, head_count, head_dim), axis=2).T
    query_all, grad_all = (
        lax.all_gather(queries, "src", axis=0, tiled=True),
        lax.all_gather(out_grad, "src", axis=0, tiled=True),
    )
    norm_all, delta_all = (
        lax.all_gather(log_norms, "src", axis=1, tiled=True),
        lax.all_gather(row_delta, "src", axis=1, tiled=True),
    )
    group_rows = query_all.shape[0]
    dest_blocks = group_rows // block_len
    query_blk = query_all.reshape(dest_blocks, block_len, head_count, head_dim)
    grad_blk = grad_all.reshape(dest_blocks, block_len, head_count, head_dim)
    norm_blk = norm_all.reshape(head_count, dest_blocks, block_len).transpose(1, 0, 2)
    delta_blk = delta_all.reshape(head_count, dest_blocks, block_len).transpose(1, 0, 2)
    key_blk = src_keys.reshape(-1, block_len, head_count, head_dim)
    value_blk = src_values.reshape(-1, block_len, head_count, head_dim)
    src_blocks = key_blk.shape[0]
    dest_idx = block_list[0, 0, 0]
    src_idx = block_list[0, 0, 1]
    capacity = dest_idx.shape[0]
    alive_rows = (jnp.arange(capacity, dtype=jnp.int32) < block_count[0, 0]).astype(jnp.float32)
    batch_size = 4
    turn_count = capacity // batch_size
    sweep_inputs = (
        dest_idx.reshape(turn_count, batch_size),
        src_idx.reshape(turn_count, batch_size),
        mask_bits[0, 0].reshape(turn_count, batch_size, -1, block_len),
        alive_rows.reshape(turn_count, batch_size),
    )

    def visit_blocks(totals, slices):
        query_total, key_total, value_total = totals
        dest_pick, src_pick, packed, alive_pick = slices
        edge_mask = unpack_mask(packed).astype(jnp.float32) * alive_pick[:, None, None]
        query_rows = query_blk[dest_pick]
        grad_rows = grad_blk[dest_pick]
        key_rows = key_blk[src_pick]
        value_rows = value_blk[src_pick]
        scores = (
            jnp.einsum("cihd,cjhd->chij", query_rows, key_rows, preferred_element_type=jnp.float32)
            * score_scale
        )
        attn_probs = jnp.exp(scores - norm_blk[dest_pick][..., None]) * edge_mask[:, None]
        prob_grad = jnp.einsum(
            "cihd,cjhd->chij", grad_rows, value_rows, preferred_element_type=jnp.float32
        )
        score_grad = attn_probs * (prob_grad - delta_blk[dest_pick][..., None])
        score_low = score_grad.astype(jnp.bfloat16)
        value_part = jnp.einsum(
            "chij,cihd->cjhd",
            attn_probs.astype(jnp.bfloat16),
            grad_rows,
            preferred_element_type=jnp.float32,
        )
        key_part = (
            jnp.einsum("chij,cihd->cjhd", score_low, query_rows, preferred_element_type=jnp.float32)
            * score_scale
        )
        key_total = key_total.at[src_pick].add(key_part)
        value_total = value_total.at[src_pick].add(value_part)
        query_part = (
            jnp.einsum("chij,cjhd->cihd", score_low, key_rows, preferred_element_type=jnp.float32)
            * score_scale
        )
        query_total = query_total.at[dest_pick].add(query_part)
        return ((query_total, key_total, value_total), None)

    initial = (
        jnp.zeros((dest_blocks, block_len, head_count, head_dim), jnp.float32),
        jnp.zeros((src_blocks, block_len, head_count, head_dim), jnp.float32),
        jnp.zeros((src_blocks, block_len, head_count, head_dim), jnp.float32),
    )
    query_total, key_total, value_total = lax.scan(visit_blocks, initial, sweep_inputs)[0]
    key_grad = lax.psum_scatter(
        key_total.reshape(-1, features), "rep", scatter_dimension=0, tiled=True
    ).astype(jnp.bfloat16)
    value_grad = lax.psum_scatter(
        value_total.reshape(-1, features), "rep", scatter_dimension=0, tiled=True
    ).astype(jnp.bfloat16)
    query_grad = lax.psum_scatter(
        query_total.reshape(group_rows, features), "src", scatter_dimension=0, tiled=True
    ).astype(jnp.bfloat16)
    return (query_grad, key_grad, value_grad)


def solution(mesh):
    placed = (
        P(("src", "rep"), None),
        P(("src", "rep"), None),
        P(("src", "rep"), None),
        P(None, ("src", "rep")),
        P("src", None),
        P("src", None),
        P("src", "rep", None, None),
        P("src", "rep"),
        P("src", "rep", None, None, None),
    )
    return jax.shard_map(
        shards,
        mesh=mesh,
        in_specs=placed,
        out_specs=(P(("src", "rep"), None), P(("src", "rep"), None), P(("src", "rep"), None)),
        check_vma=False,
    )
```

profile of v0, /device:TPU:0, one launch (start us, length us, event | category | flops | bytes accessed | tf_op | source)
XLA Modules:
  0.0 1076.1 jit_solution(2113493605998217753)
XLA Ops:
  11.7 28.7 %all_gather.15 = f32[4,2048]{0,1:T(8,128)S(1)} all-gather(f32[4,128]{0,1:T(8,128)S(1)} %bitcast.107), channel_id=1, replica_groups=mesh['src'=16,'rep'=8] {'src'}, dimensions={1}, use_global_device_ids=true | all-gather | bytes 34816 | tf_op jit(solution)/shard_map/all_gather | solution.py:32
  43.0 19.6 %all_gather.13 = f32[4,2048]{1,0:T(4,128)S(1)} all-gather(f32[4,128]{1,0:T(4,128)S(1)} %copy-done.4), channel_id=1, replica_groups=mesh['src'=16,'rep'=8] {'src'}, dimensions={1}, use_global_device_ids=true | all-gather | bytes 34816 | tf_op jit(solution)/shard_map/all_gather | solution.py:31
  62.6 4.0 reshape.112
  66.6 43.6 %all-gather.5.cloned.1.call-done = bf16[2048,512]{1,0:T(8,128)(2,1)} async-done(((bf16[128,512]{1,0:T(8,128)(2,1)}), bf16[2048,512]{1,0:T(8,128)(2,1)}) %all-gather.5.cloned.1.call-update) | async-done | bytes 2097168 | tf_op jit(solution)/shard_map/all_gather | solution.py:28
  110.2 4.0 reshape.114
  119.8 774.0 %while.14 = (s32[]{:T(128)}, f32[16,128,4,128]{3,1,2,0:T(8,128)}, f32[8,128,4,128]{3,1,2,0:T(8,128)}, f32[8,128,4,128]{3,1,2,0:T(8,128)}, s32[24,4]{1,0:T(8,128)...) while((s32[]{:T(128)}, f32[16,128,4,128]{3,1,2,0:T(8,128)}, ...), condition=%wide.region_5.6_spmd, body=%wide.region_1.5_spmd.sunk | while | flops 338954272 | bytes 39430620 | solution.py:98
  142.3 3.4 scatter_fusion.1
  174.5 3.4 scatter_fusion.1
  206.7 3.5 scatter_fusion.1
  239.0 3.5 scatter_fusion.1
  271.2 3.4 scatter_fusion.1
  303.4 3.4 scatter_fusion.1
  335.5 3.4 scatter_fusion.1
  367.7 3.5 scatter_fusion.1
  400.1 3.6 scatter_fusion.1
  432.6 3.5 scatter_fusion.1
  465.0 3.6 scatter_fusion.1
  497.3 3.4 scatter_fusion.1
  529.5 3.5 scatter_fusion.1
  561.9 3.5 scatter_fusion.1
  594.1 3.5 scatter_fusion.1
  626.5 3.5 scatter_fusion.1
  658.9 3.5 scatter_fusion.1
  691.1 3.4 scatter_fusion.1
  723.3 3.6 scatter_fusion.1
  819.7 3.5 scatter_fusion.1
  851.9 3.4 scatter_fusion.1
  884.1 3.4 scatter_fusion.1
  902.8 5.0 copy.51
  910.2 30.2 %reduce-scatter.8.cloned.1.call-done = f32[128,512]{1,0:T(8,128)} async-done(((f32[1024,512]{1,0:T(8,128)}), f32[128,512]{1,0:T(8,128)}) %reduce-scatter.8.cloned.1.call-update) | async-done | bytes 262160 | tf_op jit(solution)/shard_map/reduce_scatter | solution.py:102
  941.9 42.4 %reduce-scatter.6.cloned.1.call-done = f32[128,512]{1,0:T(8,128)} async-done(((f32[1024,512]{1,0:T(8,128)}), f32[128,512]{1,0:T(8,128)}) %reduce-scatter.6.cloned.1.call-update) | async-done | bytes 262160 | tf_op jit(solution)/shard_map/reduce_scatter | solution.py:99
  986.0 82.0 %reduce-scatter.4.cloned.1.call-done = f32[128,512]{1,0:T(8,128)} async-done(((f32[2048,512]{1,0:T(8,128)}), f32[128,512]{1,0:T(8,128)}) %reduce-scatter.4.cloned.1.call-update) | async-done | bytes 262160 | tf_op jit(solution)/shard_map/reduce_scatter | solution.py:105
  (738 shorter events, 722.8 us)
Async XLA Ops:
  7.2 33.6 %copy-start.2 = (bf16[1024,512]{1,0:T(8,128)(2,1)S(1)}, bf16[1024,512]{1,0:T(8,128)(2,1)}, u32[]{:S(2)}) copy-start(bf16[1024,512]{1,0:T(8,128)(2,1)} %param.15) | copy-start | bytes 3145732
  7.2 55.4 %all-gather.3.cloned.1.call-start = ((), (), s32[]{:S(2)}) async-start(), calls=%async_computation.3 | async-start | bytes 2228224 | tf_op jit(solution)/shard_map/all_gather | solution.py:27
  7.9 102.2 %all-gather.5.cloned.1.call-start = ((), (), s32[]{:S(2)}) async-start(), calls=%async_computation.4 | async-start | bytes 2228224 | tf_op jit(solution)/shard_map/all_gather | solution.py:28
  8.7 931.7 %reduce-scatter.8.cloned.1.call-start = ((), (), s32[]{:S(2)}) async-start(), calls=%async_computation.7 | async-start | bytes 2359296 | tf_op jit(solution)/shard_map/reduce_scatter | solution.py:102
  11.6 30.3 %copy-start.3 = (bf16[1024,512]{1,0:T(8,128)(2,1)S(1)}, bf16[1024,512]{1,0:T(8,128)(2,1)}, u32[]{:S(2)}) copy-start(bf16[1024,512]{1,0:T(8,128)(2,1)} %param.16) | copy-start | bytes 3145732
  40.7 2.3 copy-start.4
  139.3 1.7 copy-start
  171.5 1.7 copy-start
  203.7 1.7 copy-start
  236.0 1.7 copy-start
  268.3 1.7 copy-start
  300.4 1.7 copy-start
  332.5 1.7 copy-start
  364.8 1.7 copy-start
  397.1 1.7 copy-start
  429.6 1.7 copy-start
  462.0 1.7 copy-start
  494.4 1.7 copy-start
  526.5 1.7 copy-start
  558.9 1.7 copy-start
  591.2 1.7 copy-start
  623.5 1.7 copy-start
  655.9 1.7 copy-start
  688.1 1.7 copy-start
  720.3 1.7 copy-start
  752.7 1.7 copy-start
  784.6 1.7 copy-start
  816.7 1.7 copy-start
  848.9 1.7 copy-start
  881.1 1.7 copy-start
  898.3 86.1 %reduce-scatter.6.cloned.1.call-start = ((), (), s32[]{:S(2)}) async-start(), calls=%async_computation.6 | async-start | bytes 2359296 | tf_op jit(solution)/shard_map/reduce_scatter | solution.py:99
  902.7 165.2 %reduce-scatter.4.cloned.1.call-start = ((), (), s32[]{:S(2)}) async-start(), calls=%async_computation.5 | async-start | bytes 4456448 | tf_op jit(solution)/shard_map/reduce_scatter | solution.py:105
  (1 other events, 1.6 us)
Sparse Core Ops, SparseCore 0:
  10.4 50.7 all-gather.2
  63.7 46.4 all-gather.4
  898.4 41.8 reduce-scatter.7
  942.6 41.7 reduce-scatter.5
  988.2 79.7 reduce-scatter.3
where the time goes:
time: 1080 us
  local copies, waits for them, and re-layouts  441 us (41%)
  other arithmetic  242 us (22%)
  waiting for transfers between devices  200 us (19%)
  matrix products  128 us (12%)
  blocking collectives  48.3 us (4%)
  between operations  14.5 us (1%)
    scatter-add x24, other arithmetic, visit_blocks(): key_total = key_total.at[src_pick].add(key_part)  83.4 us
    reduce_scatter x1, waiting for transfers between devices, shards(): lax.psum_scatter(query_total.reshape(group_rows, features), 'src', scatte...  82 us
    scatter-add x24, other arithmetic, visit_blocks(): query_total = query_total.at[dest_pick].add(query_part)  75.1 us
    scatter-add x24, other arithmetic, visit_blocks(): value_total = value_total.at[src_pick].add(value_part)  74.5 us
    gather x48, local copies, waits for them, and re-layouts, visit_blocks(): query_rows = query_blk[dest_pick]  69.3 us
    gather x48, local copies, waits for them, and re-layouts, visit_blocks(): grad_rows = grad_blk[dest_pick]  69.3 us
    gather x48, local copies, waits for them, and re-layouts, visit_blocks(): key_rows = key_blk[src_pick]  60.4 us
    gather x24, local copies, waits for them, and re-layouts, visit_blocks(): value_rows = value_blk[src_pick]  53.2 us
  transfers between devices with their start and end apart: 5, of which 4 were waited for; matrix products, arithmetic and copies ran while one was open for 2% of the time, Pallas kernels for 0%

commit v1 on v0

v1 whole, which is shorter than its diff:
```python
import functools
import math

import jax
import jax.numpy as jnp
from jax import lax
from jax.experimental import pallas as pl
from jax.experimental.pallas import tpu as pltpu
from jax.sharding import PartitionSpec as P

F32 = jnp.float32
BF16 = jnp.bfloat16
LOG2E = math.log2(math.e)


def nt_dot(a, b):
    return lax.dot_general(a, b, (((1,), (1,)), ((), ())), preferred_element_type=F32)


def nn_dot(a, b):
    return lax.dot_general(a, b, (((1,), (0,)), ((), ())), preferred_element_type=F32)


def tn_dot(a, b):
    return lax.dot_general(a, b, (((0,), (0,)), ((), ())), preferred_element_type=F32)


def build_masks(dst_blocks, src_blocks, table, words_ref, mask_ref):
    row = lax.broadcasted_iota(jnp.int32, (16, 128), 0)
    lane = lax.broadcasted_iota(jnp.int32, (16, 128), 1)
    half = jnp.where(lax.rem(lane, 16) >= 8, 8, 0)
    spread = jnp.where(row == lane // 16 + half, 1.0, 0.0).astype(BF16)
    bit = jnp.left_shift(1, lax.rem(lax.broadcasted_iota(jnp.int32, (1, 128), 1), 8))

    def one_dest(t, carry):
        words = jnp.concatenate(
            [
                words_ref[table[0, t * src_blocks + j]] * table[1, t * src_blocks + j]
                for j in range(src_blocks)
            ],
            axis=1,
        )
        halves = jnp.concatenate(
            [jnp.bitwise_and(words, 255), jnp.bitwise_and(jnp.right_shift(words, 8), 255)], axis=0
        )
        wide = tn_dot(halves.astype(F32).astype(BF16), spread).astype(jnp.int32)
        picked = jnp.where(jnp.bitwise_and(wide, bit) != 0, 1.0, 0.0)
        mask_ref[:, pl.ds(pl.multiple_of(t * 128, 128), 128)] = picked
        return carry

    lax.fori_loop(0, dst_blocks, one_dest, 0)


def visit(scale, rows, tile, q, g, norm, delta, k_ref, v_ref, kt, mask_ref, at, dk_ref, dv_ref, pbuf, sbuf):
    n_src = k_ref.shape[0]
    for c in range(n_src // tile):
        cs = pl.ds(c * tile, tile)
        s = nt_dot(k_ref[cs, :], q)
        e = jnp.exp2(s * (scale * LOG2E) - norm)
        p = e * mask_ref[cs, pl.ds(at, rows)]
        d = nt_dot(v_ref[cs, :], g)
        ds = p * (d - delta)
        p_low = p.astype(BF16)
        s_low = ds.astype(BF16)
        sbuf[cs, :] = s_low
        dv_ref[cs, :] += nn_dot(p_low, g)
        dk_ref[cs, :] += nn_dot(s_low, q)
    return nn_dot(kt, sbuf[...])


def core(heads, rows, tile, table, words_ref, q_hbm, g_hbm, nd_ref, k_hbm, v_hbm, dq_ref, dk_ref, dv_ref,
         mask_ref, q_all, g_all, k_all, v_all, kt, pbuf, sbuf, sems):
    n_dst, hd = q_all.shape[1:]
    copies = []
    for h in range(heads):
        cols = pl.ds(h * hd, hd)
        for i, (a, b) in enumerate(((q_hbm, q_all), (g_hbm, g_all), (k_hbm, k_all), (v_hbm, v_all))):
            cp = pltpu.make_async_copy(a.at[:, cols], b.at[h], sems.at[h, i])
            cp.start()
            copies.append(cp)
    build_masks(n_dst // 128, k_all.shape[1] // 128, table, words_ref, mask_ref)
    for cp in copies:
        cp.wait()
    scale = hd ** -0.5
    dk_ref[...] = jnp.zeros_like(dk_ref)
    dv_ref[...] = jnp.zeros_like(dv_ref)

    def one_head(h, carry):
        kt[...] = k_all[h].T

        def one_chunk(i, carry):
            at = pl.multiple_of(i * rows, rows)
            q = q_all[h, pl.ds(at, rows), :]
            g = g_all[h, pl.ds(at, rows), :]
            norm = nd_ref[h, 0:1, pl.ds(at, rows)] * LOG2E
            delta = nd_ref[h, 1:2, pl.ds(at, rows)]
            dqt = visit(scale, rows, tile, q, g, norm, delta, k_all.at[h], v_all.at[h], kt[...], mask_ref, at,
                        dk_ref.at[h], dv_ref.at[h], pbuf, sbuf)
            dq_ref[h, pl.ds(at, rows), :] = dqt.T * scale
            return carry

        lax.fori_loop(0, n_dst // rows, one_chunk, 0)
        dk_ref[h] = dk_ref[h] * scale
        return carry

    lax.fori_loop(0, heads, one_head, 0)


def attention(heads, q, g, norm, delta, k, v, table, words):
    n_dst, features = q.shape
    n_src = k.shape[0]
    hd = features // heads
    nd = jnp.stack([norm, delta], axis=1)
    rows, tile = 512, 128
    vmem = pl.BlockSpec(memory_space=pltpu.VMEM)
    anyspace = pl.BlockSpec(memory_space=pl.ANY)
    return pl.pallas_call(
        functools.partial(core, heads, rows, tile),
        out_shape=(
            jax.ShapeDtypeStruct((heads, n_dst, hd), F32),
            jax.ShapeDtypeStruct((heads, n_src, hd), F32),
            jax.ShapeDtypeStruct((heads, n_src, hd), F32),
        ),
        in_specs=[pl.BlockSpec(memory_space=pltpu.SMEM), vmem, anyspace, anyspace, vmem, anyspace, anyspace],
        out_specs=(vmem, vmem, vmem),
        scratch_shapes=[
            pltpu.VMEM((n_src, n_dst), F32),
            pltpu.VMEM((heads, n_dst, hd), BF16),
            pltpu.VMEM((heads, n_dst, hd), BF16),
            pltpu.VMEM((heads, n_src, hd), BF16),
            pltpu.VMEM((heads, n_src, hd), BF16),
            pltpu.VMEM((hd, n_src), BF16),
            pltpu.VMEM((8, 128), BF16),
            pltpu.VMEM((n_src, rows), BF16),
            pltpu.SemaphoreType.DMA((heads, 4)),
        ],
        compiler_params=pltpu.CompilerParams(vmem_limit_bytes=56 << 20),
        name="attention",
    )(table, words, q, g, nd, k, v)


def pair_table(block_list, block_count, n_pairs, src_blocks):
    capacity = block_list.shape[1]
    order = jnp.arange(capacity, dtype=jnp.int32)
    code = block_list[0] * src_blocks + block_list[1]
    hit = (code[:, None] == jnp.arange(n_pairs, dtype=jnp.int32)) & (order < block_count)[:, None]
    slot = jnp.sum(jnp.where(hit, order[:, None], 0), axis=0)
    live = jnp.sum(hit.astype(jnp.int32), axis=0)
    return jnp.stack([slot, live])


def shards(queries, out_grad, outputs, log_norms, src_keys, src_values, block_list, block_count, mask_bits):
    heads = log_norms.shape[0]
    features = queries.shape[1]
    hd = features // heads
    local = queries.shape[0]
    block = mask_bits.shape[-1]
    products = out_grad.astype(F32) * outputs.astype(F32)
    row_delta = jnp.sum(products.reshape(local, heads, hd), axis=2).T
    q_all = lax.all_gather(queries, "src", axis=0, tiled=True)
    g_all = lax.all_gather(out_grad, "src", axis=0, tiled=True)
    norm_all = lax.all_gather(log_norms, "src", axis=1, tiled=True)
    delta_all = lax.all_gather(row_delta, "src", axis=1, tiled=True)
    src_blocks = src_keys.shape[0] // block
    table = pair_table(block_list[0, 0], block_count[0, 0], q_all.shape[0] // block * src_blocks, src_blocks)
    dq, dk, dv = attention(heads, q_all, g_all, norm_all, delta_all, src_keys, src_values, table, mask_bits[0, 0])

    def spread(x, axis):
        x = lax.psum_scatter(x, axis, scatter_dimension=1, tiled=True)
        return x.transpose(1, 0, 2).reshape(-1, features).astype(BF16)

    return spread(dq, "src"), spread(dk, "rep"), spread(dv, "rep")


def solution(mesh):
    rows = P(("src", "rep"), None)
    placed = (
        rows,
        rows,
        rows,
        P(None, ("src", "rep")),
        P("src", None),
        P("src", None),
        P("src", "rep", None, None),
        P("src", "rep"),
        P("src", "rep", None, None, None),
    )
    return jax.shard_map(shards, mesh=mesh, in_specs=placed, out_specs=(rows, rows, rows), check_vma=False)
```

time: 1080 us -> 333 us (0.31)
  local copies, waits for them, and re-layouts: 441 us -> 2.92 us
  other arithmetic: 242 us -> 6.26 us
  matrix products: 128 us -> 0 us
  Pallas kernels: 0 us -> 45.1 us
  waiting for transfers between devices: 200 us -> 218 us
    gather x216 -> x0, local copies, waits for them, and re-layouts: 280 us -> none  [the longest x48 69.3 us: visit_blocks(): query_rows = query_blk[dest_pick]]
    scatter-add x72 -> x0, other arithmetic: 233 us -> none  [the longest x24 83.4 us: visit_blocks(): key_total = key_total.at[src_pick].add(key_part)]
    dot_general x120 -> x0, matrix products: 128 us -> none  [the longest x24 35.5 us: visit_blocks(): jnp.einsum('chij,cjhd->cihd', score_low, key_rows, preferred_element_type...]
    mul x72 -> x0, local copies, waits for them, and re-layouts: 71.2 us -> none  [the longest x24 39.4 us: visit_blocks(): jnp.einsum('chij,cjhd->cihd', score_low, key_rows, preferred_element_type...]
    pallas_call x0 -> x1, Pallas kernels: none -> 45.1 us  [attention(): pl.pallas_call(functools.partial(core, heads, rows, tile), out_shape=(jax...]
    transpose x24 -> x0, local copies, waits for them, and re-layouts: 37.3 us -> none  [visit_blocks(): jnp.einsum('chij,cihd->cjhd', attn_probs.astype(jnp.bfloat16), grad_rows,...]
    shift_right_arithmetic x72 -> x0, local copies, waits for them, and re-layouts: 19.3 us -> none  [unpack_mask(): jnp.right_shift(packed[..., :, None, :], shifts[:, None])]
  transfers between devices with their start and end apart: 5 -> 5, of which waited for: 4 -> 5; matrix products, arithmetic and copies ran while one was open for 2% -> 2% of each run, Pallas kernels for 0% -> 0%
where the time goes in v1:
time: 333 us; the launch traced here: 332 us
  waiting for transfers between devices  218 us (65%)
  blocking collectives  45.6 us (14%)
  Pallas kernels  45.1 us (14%)
  between operations  14.5 us (4%)
  other arithmetic  6.26 us (2%)
    reduce_scatter x3, waiting for transfers between devices, spread(): x = lax.psum_scatter(x, axis, scatter_dimension=1, tiled=True)  165 us
    all_gather x1, waiting for transfers between devices, shards(): g_all = lax.all_gather(out_grad, 'src', axis=0, tiled=True)  48.7 us
    pallas_call x1, Pallas kernels, attention(): pl.pallas_call(functools.partial(core, heads, rows, tile), out_shape=(jax...  45.1 us
    all_gather x1, blocking collectives, shards(): norm_all = lax.all_gather(log_norms, 'src', axis=1, tiled=True)  26 us
    all_gather x1, blocking collectives, shards(): delta_all = lax.all_gather(row_delta, 'src', axis=1, tiled=True)  19.6 us
  transfers between devices with their start and end apart: 5, of which 5 were waited for; matrix products, arithmetic and copies ran while one was open for 2% of the time, Pallas kernels for 0%

profile of v1, /device:TPU:0, one launch (start us, length us, event | category | flops | bytes accessed | tf_op | source)
XLA Modules:
  0.0 332.4 jit_solution(1446148046519891478)
XLA Ops:
  7.2 0.7 all-gather.3.cloned.1.call-update
  7.9 0.7 all-gather.5.cloned.1.call-update
  8.6 0.0 reduce-scatter.6.cloned.1.call-start
  9.3 26.0 %all_gather.14 = f32[4,2048]{1,0:T(4,128)S(1)} all-gather(f32[4,128]{1,0:T(4,128)} %param.12), channel_id=1, replica_groups=mesh['src'=16,'rep'=8] {'src'}, dimensions={1}, use_global_device_ids=true | all-gather | bytes 34816 | tf_op jit(solution)/shard_map/all_gather | solution.py:162
  35.4 1.0 convert_multiply_fusion
  36.4 0.1 reshape.36
  36.5 0.2 reduce_sum.29
  36.7 0.1 copy.25
  36.8 19.6 %all_gather.15 = f32[4,2048]{1,0:T(4,128)S(1)} all-gather(f32[4,128]{1,0:T(4,128)S(1)} %bitcast.21), channel_id=1, replica_groups=mesh['src'=16,'rep'=8] {'src'}, dimensions={1}, use_global_device_ids=true | all-gather | bytes 34816 | tf_op jit(solution)/shard_map/all_gather | solution.py:163
  56.4 0.8 add_bitcast_fusion
  57.2 0.1 select_reduce_fusion
  57.3 0.6 pad_add_fusion.table
  57.9 0.7 pad_maximum_fusion.nd_ref
  58.6 2.0 all-gather.3.cloned.1.call-done.q_hbm
  60.6 48.7 %all-gather.5.cloned.1.call-done.g_hbm = bf16[2048,512]{1,0:T(8,128)(2,1)} async-done(((bf16[128,512]{1,0:T(8,128)(2,1)}), bf16[2048,512]{1,0:T(8,128)(2,1)}) %all-gather.5.cloned.1.call-update) | async-done | bytes 2097168 | tf_op jit(solution)/shard_map/all_gather | solution.py:161
  109.4 45.1 %attention.1 = (f32[4,2048,128]{2,1,0:T(8,128)}, f32[4,1024,128]{2,1,0:T(8,128)}, f32[4,1024,128]{2,1,0:T(8,128)}) custom-call(s32[2,128]{1,0:T(2,128)} %pad_add_fusion.table, s32[96,8,128]{2,1,0:T(8,128)} %bitcast.20, bf16[2048,512]{1,0:T(8,128)(2,1)} %all-gather.3.cloned.1.call-done.q_hbm, bf16[2048,512]{1,0:T(8,128)(2,1)} %all-gather.5.cloned.1.call-done.g_hbm, ...), custom_call_target="tpu_custom_call" | custom-call | tf_op jit(solution)/shard_map/attention/pallas_call | solution.py:117
  154.5 0.0 reduce-scatter.8.cloned.1.call-start
  154.6 0.5 reduce-scatter.8.cloned.1.call-update
  155.1 0.0 reduce-scatter.4.cloned.1.call-start
  155.1 0.5 reduce-scatter.4.cloned.1.call-update
  155.7 40.6 %reduce-scatter.6.cloned.1.call-done = f32[4,128,128]{2,1,0:T(8,128)} async-done(((f32[4,1024,128]{2,1,0:T(8,128)}), f32[4,128,128]{2,1,0:T(8,128)}) %reduce-scatter.6.cloned.1.call-update) | async-done | bytes 262160 | tf_op jit(solution)/shard_map/reduce_scatter | solution.py:169
  196.3 1.0 convert_bitcast_fusion.1
  197.3 0.1 copy.27
  197.4 0.8 copy.30
  198.2 42.1 %reduce-scatter.8.cloned.1.call-done = f32[4,128,128]{2,1,0:T(8,128)} async-done(((f32[4,1024,128]{2,1,0:T(8,128)}), f32[4,128,128]{2,1,0:T(8,128)}) %reduce-scatter.8.cloned.1.call-update) | async-done | bytes 262160 | tf_op jit(solution)/shard_map/reduce_scatter | solution.py:169
  240.4 1.0 convert_bitcast_fusion
  241.3 0.1 copy.28
  241.5 0.8 copy.31
  242.2 81.7 %reduce-scatter.4.cloned.1.call-done = f32[4,128,128]{2,1,0:T(8,128)} async-done(((f32[4,2048,128]{2,1,0:T(8,128)}), f32[4,128,128]{2,1,0:T(8,128)}) %reduce-scatter.4.cloned.1.call-update) | async-done | bytes 262160 | tf_op jit(solution)/shard_map/reduce_scatter | solution.py:169
  324.0 1.0 convert_bitcast_fusion.2
  324.9 0.1 copy.26
  325.1 0.8 copy.29
  (6 shorter events, 0.1 us)
Async XLA Ops:
  7.2 53.4 %all-gather.3.cloned.1.call-start = ((), (), s32[]{:S(2)}) async-start(), calls=%async_computation.3 | async-start | bytes 2228224 | tf_op jit(solution)/shard_map/all_gather | solution.py:160
  7.9 101.5 %all-gather.5.cloned.1.call-start = ((), (), s32[]{:S(2)}) async-start(), calls=%async_computation.4 | async-start | bytes 2228224 | tf_op jit(solution)/shard_map/all_gather | solution.py:161
  8.6 187.7 %reduce-scatter.6.cloned.1.call-start = ((), (), s32[]{:S(2)}) async-start(), calls=%async_computation.6 | async-start | bytes 2359296 | tf_op jit(solution)/shard_map/reduce_scatter | solution.py:169
  154.5 85.8 %reduce-scatter.8.cloned.1.call-start = ((), (), s32[]{:S(2)}) async-start(), calls=%async_computation.7 | async-start | bytes 2359296 | tf_op jit(solution)/shard_map/reduce_scatter | solution.py:169
  155.1 168.9 %reduce-scatter.4.cloned.1.call-start = ((), (), s32[]{:S(2)}) async-start(), calls=%async_computation.5 | async-start | bytes 4456448 | tf_op jit(solution)/shard_map/reduce_scatter | solution.py:169
Sparse Core Ops, SparseCore 0:
  10.4 50.1 all-gather.2
  63.1 46.2 all-gather.4
  154.6 41.6 reduce-scatter.5
  198.6 41.7 reduce-scatter.7
  244.2 79.6 reduce-scatter.3

commit v2 on v1

v2 whole, which is shorter than its diff:
```python
import functools
import math

import jax
import jax.numpy as jnp
from jax import lax
from jax.experimental import pallas as pl
from jax.experimental.pallas import tpu as pltpu
from jax.sharding import PartitionSpec as P

F32 = jnp.float32
BF16 = jnp.bfloat16
LOG2E = math.log2(math.e)
MESH = pl.DeviceIdType.MESH


def nt_dot(a, b):
    return lax.dot_general(a, b, (((1,), (1,)), ((), ())), preferred_element_type=F32)


def nn_dot(a, b):
    return lax.dot_general(a, b, (((1,), (0,)), ((), ())), preferred_element_type=F32)


def tn_dot(a, b):
    return lax.dot_general(a, b, (((0,), (0,)), ((), ())), preferred_element_type=F32)


def build_masks(u, dest, src_blocks, table, words_ref, mask_ref):
    row = lax.broadcasted_iota(jnp.int32, (16, 128), 0)
    lane = lax.broadcasted_iota(jnp.int32, (16, 128), 1)
    half = jnp.where(lax.rem(lane, 16) >= 8, 8, 0)
    spread = jnp.where(row == lane // 16 + half, 1.0, 0.0).astype(BF16)
    bit = jnp.left_shift(1, lax.rem(lax.broadcasted_iota(jnp.int32, (1, 128), 1), 8))
    words = jnp.concatenate(
        [
            words_ref[table[0, dest * src_blocks + j]] * table[1, dest * src_blocks + j]
            for j in range(src_blocks)
        ],
        axis=1,
    )
    halves = jnp.concatenate(
        [jnp.bitwise_and(words, 255), jnp.bitwise_and(jnp.right_shift(words, 8), 255)], axis=0
    )
    wide = tn_dot(halves.astype(F32).astype(BF16), spread).astype(jnp.int32)
    picked = jnp.where(jnp.bitwise_and(wide, bit) != 0, 1.0, 0.0)
    mask_ref[:, pl.ds(pl.multiple_of(u * 128, 128), 128)] = picked


def visit(scale, tile, q, g, norm, delta, k_ref, v_ref, kt, mask_ref, at, dk_ref, dv_ref, sbuf):
    n_src = k_ref.shape[0]
    rows = q.shape[0]
    for c in range(n_src // tile):
        cs = pl.ds(c * tile, tile)
        s = nt_dot(k_ref[cs, :], q)
        e = jnp.exp2(s * (scale * LOG2E) - norm)
        p = e * mask_ref[cs, pl.ds(at, rows)]
        d = nt_dot(v_ref[cs, :], g)
        ds = p * (d - delta)
        p_low = p.astype(BF16)
        s_low = ds.astype(BF16)
        sbuf[cs, :] = s_low
        dv_ref[cs, :] += nn_dot(p_low, g)
        dk_ref[cs, :] += nn_dot(s_low, q)
    return nn_dot(kt, sbuf[...])


def core(heads, tile, table, words_ref, q_hbm, g_hbm, nd_hbm, k_hbm, v_hbm, dq_ref, dk_ref, dv_ref,
         mask_ref, qg, nd, k_all, v_all, kt, sbuf, dk_acc, dv_acc,
         send_a, recv_a, acc_a, send_b, recv_b, tot_c, send_c, recv_c,
         send_x, recv_x, keep_x, tot_y, send_y, recv_y,
         local_sem, ag_send, ag_recv, nd_send, nd_recv, rs_send, rs_recv):
    hd = kt.shape[0]
    n_src = kt.shape[1]
    rows = 4 * 128
    scale = hd ** -0.5
    src, rep = lax.axis_index("src"), lax.axis_index("rep")
    yh, z, c = src // 8, lax.rem(src, 8) // 2, lax.rem(src, 2)
    yl, x = rep // 4, lax.rem(rep, 4)

    def at_src(yy, zz, cc):
        return {"src": yy * 8 + zz * 2 + cc, "rep": rep}

    def at_rep(yy, xx):
        return {"src": src, "rep": yy * 4 + xx}

    sibling = at_src(yh, z, 1 - c)
    across = at_src(1 - yh, z, c)
    zs = [lax.rem(z + d, 4) for d in (1, 2, 3)]
    xs = [lax.rem(x + d, 4) for d in (1, 2, 3)]
    around = [at_src(yh, zz, c) for zz in zs]
    beside = [at_rep(yl, xx) for xx in xs]
    over = at_rep(1 - yl, x)

    first = []
    nd_copy = pltpu.make_async_copy(nd_hbm, nd.at[c, yh, z], local_sem.at[heads, 0])
    nd_copy.start()
    for h in range(heads):
        cols = pl.ds(h * hd, hd)
        for i, (a, b) in enumerate((
            (q_hbm, qg.at[h, c, yh, 0, z]), (g_hbm, qg.at[h, c, yh, 1, z]),
            (k_hbm, k_all.at[h]), (v_hbm, v_all.at[h]),
        )):
            cp = pltpu.make_async_copy(a.at[:, cols], b, local_sem.at[h, i])
            cp.start()
            first.append((i, cp))

    barrier = pltpu.get_barrier_semaphore()
    for peer in [sibling, across, over] + around + beside:
        pl.semaphore_signal(barrier, inc=1, device_id=peer, device_id_type=MESH)
    pl.semaphore_wait(barrier, 9)

    nd_copy.wait()
    for i, cp in first:
        if i < 2:
            cp.wait()

    def remote(a, b, s, r, peer):
        return pltpu.make_async_remote_copy(
            src_ref=a, dst_ref=b, send_sem=s, recv_sem=r, device_id=peer, device_id_type=MESH
        )

    def block(h, cc, yy, zz):
        return qg.at[h, cc, yy, :, zz] if h is not None else nd.at[cc, yy, zz]

    def gather(h, slot):
        if slot == 0:
            yy, zz, peer = yh, z, across
        elif slot < 4:
            yy, zz, peer = yh, z, around[slot - 1]
        elif slot < 7:
            yy, zz, peer = 1 - yh, z, around[slot - 4]
        elif slot == 7:
            yy, zz, peer = yh, z, sibling
        elif slot == 8:
            yy, zz, peer = 1 - yh, z, sibling
        elif slot < 12:
            yy, zz, peer = yh, zs[slot - 9], sibling
        else:
            yy, zz, peer = 1 - yh, zs[slot - 12], sibling
        ref = block(h, c, yy, zz)
        if h is None:
            return remote(ref, ref, nd_send.at[slot], nd_recv.at[slot], peer)
        return remote(ref, ref, ag_send.at[h, slot], ag_recv.at[h, slot], peer)

    def arrival(h, slot):
        if slot == 0:
            cc, yy, zz = c, 1 - yh, z
        elif slot < 4:
            cc, yy, zz = c, yh, lax.rem(z + 4 - slot, 4)
        elif slot < 7:
            cc, yy, zz = c, 1 - yh, lax.rem(z + 4 - (slot - 3), 4)
        elif slot == 7:
            cc, yy, zz = 1 - c, yh, z
        elif slot == 8:
            cc, yy, zz = 1 - c, 1 - yh, z
        elif slot < 12:
            cc, yy, zz = 1 - c, yh, zs[slot - 9]
        else:
            cc, yy, zz = 1 - c, 1 - yh, zs[slot - 12]
        ref = block(h, cc, yy, zz)
        if h is None:
            return remote(ref, ref, nd_send.at[slot], nd_recv.at[slot], sibling)
        return remote(ref, ref, ag_send.at[h, slot], ag_recv.at[h, slot], sibling)

    def gather_step(h, stage):
        if stage == 0:
            for slot in (1, 2, 3, 7):
                gather(h, slot).start()
            arrival(h, 0).wait_recv()
            for slot in (4, 5, 6, 8):
                gather(h, slot).start()
        elif stage == 1:
            for d in (1, 3, 2):
                arrival(h, d).wait_recv()
                gather(h, 9 + (3 - d)).start()
        elif stage == 2:
            for d in (1, 3, 2):
                arrival(h, 3 + d).wait_recv()
                gather(h, 12 + (3 - d)).start()
        else:
            for slot in range(7, 15):
                arrival(h, slot).wait_recv()

    gather(None, 0).start()
    for h in range(heads):
        gather(h, 0).start()

    def stage_a(h, y):
        return remote(send_a.at[h, y], recv_a.at[h, y], rs_send.at[h, y], rs_recv.at[h, y], sibling)

    def stage_b(h, j):
        return remote(send_b.at[h, :, zs[j]], recv_b.at[h, j], rs_send.at[h, 2 + j], rs_recv.at[h, 2 + j], around[j])

    def stage_c(h):
        return remote(send_c.at[h], recv_c.at[h], rs_send.at[h, 5], rs_recv.at[h, 5], across)

    def stage_x(h, j):
        return remote(send_x.at[h, :, :, xs[j]], recv_x.at[h, j], rs_send.at[h, 6 + j], rs_recv.at[h, 6 + j], beside[j])

    def stage_y(h):
        return remote(send_y.at[h], recv_y.at[h], rs_send.at[h, 9], rs_recv.at[h, 9], over)

    def step(n, carry):
        h = n // 4 - 1
        i = lax.rem(n, 4)
        ahead = h + 1
        done = h - 1

        @pl.when((ahead < heads) & (i == 0))
        def _():
            @pl.when(ahead == 0)
            def _():
                gather_step(None, 0)
            gather_step(ahead, 0)

        @pl.when((done >= 0) & (i == 0))
        def _():
            for j in (0, 2, 1):
                stage_x(done, j).start()
            for y in range(2):
                stage_a(done, y).wait_recv()
                total = acc_a[y] + recv_a[done, y].astype(F32)
                acc_a[y] = total
                send_b[done, y] = total.astype(BF16)
            for y in range(2):
                tot_c[y] = acc_a[y, z]
            for j in (0, 2, 1):
                stage_b(done, j).start()

        @pl.when((ahead < heads) & (i == 1))
        def _():
            @pl.when(ahead == 0)
            def _():
                gather_step(None, 1)
            gather_step(ahead, 1)

        @pl.when((ahead < heads) & (i == 2))
        def _():
            @pl.when(ahead == 0)
            def _():
                gather_step(None, 2)
            gather_step(ahead, 2)

        @pl.when((done >= 0) & (i == 2))
        def _():
            for j in range(3):
                stage_x(done, j).wait_recv()
            for s in range(2):
                for y in range(2):
                    tot_y[s, y] = (
                        keep_x[s, y]
                        + recv_x[done, 0, s, y].astype(F32)
                        + recv_x[done, 1, s, y].astype(F32)
                        + recv_x[done, 2, s, y].astype(F32)
                    )
                send_y[done, s] = tot_y[s, 1 - yl].astype(BF16)
            stage_y(done).start()
            for j in range(3):
                stage_b(done, j).wait_recv()
            for y in range(2):
                tot_c[y] = (
                    tot_c[y]
                    + recv_b[done, 0, y].astype(F32)
                    + recv_b[done, 1, y].astype(F32)
                    + recv_b[done, 2, y].astype(F32)
                )
            send_c[done] = tot_c[1 - yh].astype(BF16)
            stage_c(done).start()

        @pl.when((done >= 0) & (i == 3))
        def _():
            cols = pl.ds(pl.multiple_of(done * hd, hd), hd)
            stage_y(done).wait_recv()
            dk_ref[:, cols] = ((tot_y[0, yl] + recv_y[done, 0].astype(F32)) * scale).astype(BF16)
            dv_ref[:, cols] = (tot_y[1, yl] + recv_y[done, 1].astype(F32)).astype(BF16)
            stage_c(done).wait_recv()
            dq_ref[:, cols] = ((tot_c[yh] + recv_c[done].astype(F32)) * scale).astype(BF16)

        @pl.when(h < 0)
        def _():
            for j in range(4):
                u = i * 4 + j
                build_masks(u, lax.rem(u // 4, 2) * 8 + lax.rem(u, 4) * 2 + u // 8, n_src // 128, table, words_ref,
                            mask_ref)

        @pl.when((h >= 0) & (h < heads))
        def _():
            @pl.when((h > 0) & (i == 0))
            def _():
                gather_step(h, 3)

            @pl.when((h == 0) & (i == 2))
            def _():
                gather_step(None, 3)
                gather_step(h, 3)

            @pl.when((h == 0) & (i == 0))
            def _():
                for k, cp in first:
                    if k >= 2:
                        cp.wait()

            @pl.when(i == 0)
            def _():
                kt[...] = k_all[h].T
                dk_acc[...] = jnp.zeros_like(dk_acc)
                dv_acc[...] = jnp.zeros_like(dv_acc)

            mine = (i >= 2) ^ (h == 0)
            cc = jnp.where(mine, c, 1 - c)
            yy = lax.rem(i, 2)
            at = pl.multiple_of((cc * 2 + yy) * rows, rows)
            q = qg[h, cc, yy, 0].reshape(rows, hd)
            g = qg[h, cc, yy, 1].reshape(rows, hd)
            norm = jnp.concatenate([nd[cc, yy, j, pl.ds(h, 1), :] for j in range(4)], axis=1) * LOG2E
            delta = jnp.concatenate([nd[cc, yy, j, pl.ds(heads + h, 1), :] for j in range(4)], axis=1)
            dqt = visit(scale, tile, q, g, norm, delta, k_all.at[h], v_all.at[h], kt[...], mask_ref, at,
                        dk_acc, dv_acc, sbuf)
            dq = dqt.T.reshape(4, 128, hd)

            @pl.when(mine)
            def _():
                acc_a[yy] = dq

            @pl.when(jnp.logical_not(mine))
            def _():
                send_a[h, yy] = dq.astype(BF16)
                stage_a(h, yy).start()

            @pl.when(i == 3)
            def _():
                for s, acc in enumerate((dk_acc, dv_acc)):
                    blocks = acc[...].reshape(2, 4, 128, hd)
                    send_x[h, s] = blocks.astype(BF16)
                    for y in range(2):
                        keep_x[s, y] = acc[pl.ds(pl.multiple_of((y * 4 + x) * 128, 128), 128), :]

        return carry

    lax.fori_loop(0, (heads + 2) * 4, step, 0)

    def drain(h, carry):
        for slot in range(15):
            gather(h, slot).wait_send()
        for y in range(2):
            stage_a(h, y).wait_send()
        for j in range(3):
            stage_b(h, j).wait_send()
            stage_x(h, j).wait_send()
        stage_c(h).wait_send()
        stage_y(h).wait_send()
        return carry

    for slot in range(15):
        gather(None, slot).wait_send()
    lax.fori_loop(0, heads, drain, 0)


def attention(heads, q, g, nd, k, v, table, words):
    local, features = q.shape
    n_src = k.shape[0]
    hd = features // heads
    tile = 128
    vmem = pl.BlockSpec(memory_space=pltpu.VMEM)
    anyspace = pl.BlockSpec(memory_space=pl.ANY)
    out = jax.ShapeDtypeStruct((local, features), BF16)
    return pl.pallas_call(
        functools.partial(core, heads, tile),
        out_shape=(out, out, out),
        in_specs=[pl.BlockSpec(memory_space=pltpu.SMEM), vmem] + [anyspace] * 5,
        out_specs=(vmem, vmem, vmem),
        scratch_shapes=[
            pltpu.VMEM((n_src, 16 * 128), F32),
            pltpu.VMEM((heads, 2, 2, 2, 4, 128, hd), BF16),
            pltpu.VMEM((2, 2, 4, 2 * heads, 128), F32),
            pltpu.VMEM((heads, n_src, hd), BF16),
            pltpu.VMEM((heads, n_src, hd), BF16),
            pltpu.VMEM((hd, n_src), BF16),
            pltpu.VMEM((n_src, 512), BF16),
            pltpu.VMEM((n_src, hd), F32),
            pltpu.VMEM((n_src, hd), F32),
            pltpu.VMEM((heads, 2, 4, 128, hd), BF16),
            pltpu.VMEM((heads, 2, 4, 128, hd), BF16),
            pltpu.VMEM((2, 4, 128, hd), F32),
            pltpu.VMEM((heads, 2, 4, 128, hd), BF16),
            pltpu.VMEM((heads, 3, 2, 128, hd), BF16),
            pltpu.VMEM((2, 128, hd), F32),
            pltpu.VMEM((heads, 128, hd), BF16),
            pltpu.VMEM((heads, 128, hd), BF16),
            pltpu.VMEM((heads, 2, 2, 4, 128, hd), BF16),
            pltpu.VMEM((heads, 3, 2, 2, 128, hd), BF16),
            pltpu.VMEM((2, 2, 128, hd), F32),
            pltpu.VMEM((2, 2, 128, hd), F32),
            pltpu.VMEM((heads, 2, 128, hd), BF16),
            pltpu.VMEM((heads, 2, 128, hd), BF16),
            pltpu.SemaphoreType.DMA((heads + 1, 4)),
            pltpu.SemaphoreType.DMA((heads, 15)),
            pltpu.SemaphoreType.DMA((heads, 15)),
            pltpu.SemaphoreType.DMA((15,)),
            pltpu.SemaphoreType.DMA((15,)),
            pltpu.SemaphoreType.DMA((heads, 10)),
            pltpu.SemaphoreType.DMA((heads, 10)),
        ],
        compiler_params=pltpu.CompilerParams(
            vmem_limit_bytes=60 << 20, collective_id=0, has_side_effects=True
        ),
        name="attention",
    )(table, words, q, g, nd, k, v)


def pair_table(block_list, block_count, n_pairs, src_blocks):
    capacity = block_list.shape[1]
    order = jnp.arange(capacity, dtype=jnp.int32)
    code = block_list[0] * src_blocks + block_list[1]
    hit = (code[:, None] == jnp.arange(n_pairs, dtype=jnp.int32)) & (order < block_count)[:, None]
    slot = jnp.sum(jnp.where(hit, order[:, None], 0), axis=0)
    live = jnp.sum(hit.astype(jnp.int32), axis=0)
    return jnp.stack([slot, live])


def shards(queries, out_grad, outputs, log_norms, src_keys, src_values, block_list, block_count, mask_bits):
    heads = log_norms.shape[0]
    features = queries.shape[1]
    hd = features // heads
    local = queries.shape[0]
    block = mask_bits.shape[-1]
    products = out_grad.astype(F32) * outputs.astype(F32)
    row_delta = jnp.sum(products.reshape(local, heads, hd), axis=2).T
    nd = jnp.concatenate([log_norms, row_delta], axis=0)
    src_blocks = src_keys.shape[0] // block
    table = pair_table(block_list[0, 0], block_count[0, 0], 16 * src_blocks, src_blocks)
    return attention(heads, queries, out_grad, nd, src_keys, src_values, table, mask_bits[0, 0])


def solution(mesh):
    rows = P(("src", "rep"), None)
    placed = (
        rows,
        rows,
        rows,
        P(None, ("src", "rep")),
        P("src", None),
        P("src", None),
        P("src", "rep", None, None),
        P("src", "rep"),
        P("src", "rep", None, None, None),
    )
    return jax.shard_map(shards, mesh=mesh, in_specs=placed, out_specs=(rows, rows, rows), check_vma=False)
```

time: 333 us -> 96.6 us (0.29)
  waiting for transfers between devices: 218 us -> 0 us
  blocking collectives: 45.6 us -> 0 us
  Pallas kernels: 45.1 us -> 87.9 us
  between operations: 14.5 us -> 1.34 us
  other arithmetic: 6.26 us -> 2.5 us
    reduce_scatter x3 -> x0, waiting for transfers between devices: 165 us -> none  [spread(): x = lax.psum_scatter(x, axis, scatter_dimension=1, tiled=True)]
    all_gather x2 -> x0, waiting for transfers between devices: 50.8 us -> none  [the longest x1 48.7 us: shards(): g_all = lax.all_gather(out_grad, 'src', axis=0, tiled=True)]
    all_gather x2 -> x0, blocking collectives: 45.6 us -> none  [the longest x1 26 us: shards(): norm_all = lax.all_gather(log_norms, 'src', axis=1, tiled=True)]
    pallas_call x1, Pallas kernels: 45.1 us -> 87.9 us  [attention(): pl.pallas_call(functools.partial(core, heads, tile), out_shape=(out, out,...]
  transfers between devices with their start and end apart: 5 -> 0, of which waited for: 5 -> 0; matrix products, arithmetic and copies ran while one was open for 2% -> 0% of each run, Pallas kernels for 0% -> 0%
where the time goes in v2:
time: 96.6 us; the launch traced here: 96.4 us
  Pallas kernels  87.9 us (91%)
  local copies, waits for them, and re-layouts  4.65 us (5%)
  other arithmetic  2.5 us (3%)
  between operations  1.34 us (1%)
    pallas_call x1, Pallas kernels, attention(): pl.pallas_call(functools.partial(core, heads, tile), out_shape=(out, out,...  87.9 us
    unnamed x11, local copies, waits for them, and re-layouts  4.5 us

profile of v2, /device:TPU:0, one launch (start us, length us, event | category | flops | bytes accessed | tf_op | source)
XLA Modules:
  0.0 96.4 jit_solution(5832483210995334454)
XLA Ops:
  1.3 0.0 copy-start.3
  1.3 0.7 copy-done.3
  2.0 0.1 select_reduce_fusion
  2.1 0.6 pad_add_fusion.table
  2.7 1.0 %convert_multiply_fusion = f32[128,512]{1,0:T(8,128)S(1)} fusion(bf16[128,512]{1,0:T(8,128)(2,1)} %param.11, bf16[128,512]{1,0:T(8,128)(2,1)} %g_hbm.1), kind=kLoop, calls=%fused_computation | loop fusion | flops 196608 | bytes 524288 | tf_op jit(solution)/shard_map/mul | solution.py:428
  3.7 0.1 reshape.30
  3.8 0.2 reduce_sum.29
  4.0 0.0 copy-start.2
  4.0 0.1 copy.13
  4.0 0.6 copy-done.2
  4.7 0.6 pad_maximum_fusion.nd_hbm
  5.3 87.9 %attention.1 = (bf16[128,512]{1,0:T(8,128)(2,1)}, bf16[128,512]{1,0:T(8,128)(2,1)}, bf16[128,512]{1,0:T(8,128)(2,1)}) custom-call(s32[2,128]{1,0:T(2,128)} %pad_add_fusion.table, s32[96,8,128]{2,1,0:T(8,128)} %bitcast.8, bf16[128,512]{1,0:T(8,128)(2,1)} %q_hbm.1, bf16[128,512]{1,0:T(8,128)(2,1)} %g_hbm.1, f32[8,128]{1,0:T(8,128)} %pad_maximum_fusion.nd_hbm, ...), custom_call_target="tpu_custom_call" | custom-call | tf_op jit(solution)/shard_map/attention/pallas_call | solution.py:368
  93.2 0.0 copy-start.1
  93.2 1.6 %copy.18 = bf16[128,512]{1,0:T(8,128)(2,1)} copy(bf16[128,512]{1,0:T(8,128)(2,1)} %get-tuple-element.8) | data formatting | bytes 262144
  94.8 0.0 copy-done.1
  94.8 0.0 copy-start
  94.8 0.7 copy.19
  95.4 0.3 copy-done
  95.7 0.7 copy.20
  (2 shorter events, 0.0 us)
Async XLA Ops:
  1.3 0.7 copy-start.3
  4.0 0.7 copy-start.2
  93.2 1.6 %copy-start.1 = (bf16[128,512]{1,0:T(8,128)(2,1)S(1)}, bf16[128,512]{1,0:T(8,128)(2,1)}, u32[]{:S(2)}) copy-start(bf16[128,512]{1,0:T(8,128)(2,1)} %get-tuple-element.9) | copy-start | bytes 393220
  94.8 1.0 copy-start

commit v3 on v2

v3 whole, which is shorter than its diff:
```python
import functools
import math

import jax
import jax.numpy as jnp
from jax import lax
from jax.experimental import pallas as pl
from jax.experimental.pallas import tpu as pltpu
from jax.sharding import PartitionSpec as P

F32 = jnp.float32
BF16 = jnp.bfloat16
LOG2E = math.log2(math.e)
MESH = pl.DeviceIdType.MESH


def nt_dot(a, b):
    return lax.dot_general(a, b, (((1,), (1,)), ((), ())), preferred_element_type=F32)


def nn_dot(a, b):
    return lax.dot_general(a, b, (((1,), (0,)), ((), ())), preferred_element_type=F32)


def tn_dot(a, b):
    return lax.dot_general(a, b, (((0,), (0,)), ((), ())), preferred_element_type=F32)


def build_masks(u, dest, src_blocks, table, words_ref, mask_ref):
    row = lax.broadcasted_iota(jnp.int32, (16, 128), 0)
    lane = lax.broadcasted_iota(jnp.int32, (16, 128), 1)
    half = jnp.where(lax.rem(lane, 16) >= 8, 8, 0)
    spread = jnp.where(row == lane // 16 + half, 1.0, 0.0).astype(BF16)
    bit = jnp.left_shift(1, lax.rem(lax.broadcasted_iota(jnp.int32, (1, 128), 1), 8))
    words = jnp.concatenate(
        [
            words_ref[0, 0, jnp.clip(table[0, dest * src_blocks + j], 0, words_ref.shape[2] - 1)] * table[1, dest * src_blocks + j]
            for j in range(src_blocks)
        ],
        axis=1,
    )
    halves = jnp.concatenate(
        [jnp.bitwise_and(words, 255), jnp.bitwise_and(jnp.right_shift(words, 8), 255)], axis=0
    )
    wide = tn_dot(halves.astype(F32).astype(BF16), spread).astype(jnp.int32)
    picked = jnp.where(jnp.bitwise_and(wide, bit) != 0, 1.0, 0.0)
    mask_ref[:, pl.ds(pl.multiple_of(u * 128, 128), 128)] = picked


def visit(scale, tile, q, g, norm, delta, k_ref, v_ref, kt, mask_ref, at, dk_ref, dv_ref, sbuf):
    n_src = k_ref.shape[0]
    rows = q.shape[0]
    for c in range(n_src // tile):
        cs = pl.ds(c * tile, tile)
        s = nt_dot(k_ref[cs, :], q)
        e = jnp.exp2(s * (scale * LOG2E) - norm)
        p = e * mask_ref[cs, pl.ds(at, rows)]
        d = nt_dot(v_ref[cs, :], g)
        ds = p * (d - delta)
        p_low = p.astype(BF16)
        s_low = ds.astype(BF16)
        sbuf[cs, :] = s_low
        dv_ref[cs, :] += nn_dot(p_low, g)
        dk_ref[cs, :] += nn_dot(s_low, q)
    return nn_dot(kt, sbuf[...])


def pair_slots(list_ref, count, src_blocks, n_pairs):
    capacity = list_ref.shape[3]
    code = list_ref[0, 0, 0:1, :] * src_blocks + list_ref[0, 0, 1:2, :]
    order = lax.broadcasted_iota(jnp.int32, (n_pairs, capacity), 1)
    pair = lax.broadcasted_iota(jnp.int32, (n_pairs, capacity), 0)
    hit = (code == pair) & (order < count)
    slot = jnp.sum(jnp.where(hit, order, 0), axis=1, keepdims=True)
    live = jnp.sum(jnp.where(hit, 1, 0), axis=1, keepdims=True)
    column = lax.broadcasted_iota(jnp.int32, (n_pairs, 128), 1)
    both = jnp.where(column == 0, slot, jnp.where(column == 1, live, 0))
    return both.T[0:8]


def core(heads, tile, count_ref, list_ref, words_hbm, q_hbm, g_hbm, o_hbm, norm_hbm, k_hbm, v_hbm,
         dq_ref, dk_ref, dv_ref,
         words, slots, table, mask_ref, qg, o_all, nd, k_all, v_all, kt, sbuf, dk_acc, dv_acc,
         send_a, recv_a, acc_a, send_c, recv_c, tot_b, send_b, recv_b,
         send_x, recv_x, keep_k, send_v, recv_v, keep_v, send_y, recv_y, send_w, recv_w,
         local_sem, extra_sem, ag_send, ag_recv, nd_send, nd_recv, rs_send, rs_recv):
    hd = kt.shape[0]
    n_src = kt.shape[1]
    src_blocks = n_src // 128
    rows = 4 * 128
    scale = hd ** -0.5
    src, rep = lax.axis_index("src"), lax.axis_index("rep")
    yh, z, c = src // 8, lax.rem(src, 8) // 2, lax.rem(src, 2)
    yl, x = rep // 4, lax.rem(rep, 4)

    def at_src(yy, zz, cc):
        return {"src": yy * 8 + zz * 2 + cc, "rep": rep}

    def at_rep(yy, xx):
        return {"src": src, "rep": yy * 4 + xx}

    sibling = at_src(yh, z, 1 - c)
    across = at_src(1 - yh, z, c)
    zs = [lax.rem(z + d, 4) for d in (1, 2, 3)]
    xs = [lax.rem(x + d, 4) for d in (1, 2, 3)]
    around = [at_src(yh, zz, c) for zz in zs]
    beside = [at_rep(yl, xx) for xx in xs]
    over = at_rep(1 - yl, x)

    barrier = pltpu.get_barrier_semaphore()
    for peer in [sibling, across, over] + around + beside:
        pl.semaphore_signal(barrier, inc=1, device_id=peer, device_id_type=MESH)

    mine_copies, kv_copies = [], []
    for h in range(heads):
        cols = pl.ds(h * hd, hd)
        for i, (a, b) in enumerate((
            (q_hbm, qg.at[h, c, yh, 0, z]), (g_hbm, qg.at[h, c, yh, 1, z]), (o_hbm, o_all.at[h]),
            (k_hbm, k_all.at[h]), (v_hbm, v_all.at[h]),
        )):
            cp = pltpu.make_async_copy(a.at[:, cols], b, local_sem.at[h, i])
            if i < 3:
                cp.start()
                mine_copies.append(cp)
            else:
                kv_copies.append(cp)
    norm_copy = pltpu.make_async_copy(norm_hbm, nd.at[c, yh, z, pl.ds(0, heads)], extra_sem.at[0])
    norm_copy.start()
    words_copy = pltpu.make_async_copy(words_hbm, words, extra_sem.at[1])
    words_copy.start()
    for cp in kv_copies:
        cp.start()

    slots[...] = pair_slots(list_ref, count_ref[0, 0], src_blocks, 128)
    table_copy = pltpu.make_async_copy(slots, table, extra_sem.at[2])
    table_copy.start()

    norm_copy.wait()
    for cp in mine_copies:
        cp.wait()
    for h in range(heads):
        product = qg[h, c, yh, 1, z].astype(F32) * o_all[h].astype(F32)
        nd[c, yh, z, heads + h : heads + h + 1, :] = jnp.sum(product.T, axis=0, keepdims=True)

    def remote(a, b, s, r, peer):
        return pltpu.make_async_remote_copy(
            src_ref=a, dst_ref=b, send_sem=s, recv_sem=r, device_id=peer, device_id_type=MESH
        )

    def gather_copy(h, cc, yy, zz, slot, peer):
        if h is None:
            ref = nd.at[cc, yy, zz]
            return remote(ref, ref, nd_send.at[slot], nd_recv.at[slot], peer)
        ref = qg.at[h, cc, yy, :, zz]
        return remote(ref, ref, ag_send.at[h, slot], ag_recv.at[h, slot], peer)

    def gather(h, slot):
        if slot == 0:
            yy, zz, peer = yh, z, across
        elif slot < 4:
            yy, zz, peer = yh, z, around[slot - 1]
        elif slot < 7:
            yy, zz, peer = 1 - yh, z, around[slot - 4]
        elif slot == 7:
            yy, zz, peer = yh, z, sibling
        elif slot == 8:
            yy, zz, peer = 1 - yh, z, sibling
        elif slot < 12:
            yy, zz, peer = yh, zs[slot - 9], sibling
        else:
            yy, zz, peer = 1 - yh, zs[slot - 12], sibling
        return gather_copy(h, c, yy, zz, slot, peer)

    def arrived(h, slot):
        if slot == 0:
            cc, yy, zz = c, 1 - yh, z
        elif slot < 4:
            cc, yy, zz = c, yh, zs[3 - slot]
        elif slot < 7:
            cc, yy, zz = c, 1 - yh, zs[6 - slot]
        elif slot == 7:
            cc, yy, zz = 1 - c, yh, z
        elif slot == 8:
            cc, yy, zz = 1 - c, 1 - yh, z
        elif slot < 12:
            cc, yy, zz = 1 - c, yh, zs[slot - 9]
        else:
            cc, yy, zz = 1 - c, 1 - yh, zs[slot - 12]
        gather_copy(h, cc, yy, zz, slot, sibling).wait_recv()

    def send_own(h):
        for slot in (1, 3, 2, 7):
            gather(h, slot).start()

    def relay_across(h):
        arrived(h, 0)
        for slot in (4, 6, 5, 8):
            gather(h, slot).start()

    def forward_own_row(h):
        for d in (1, 3, 2):
            arrived(h, d)
            gather(h, 12 - d).start()

    def forward_other_row(h):
        for d in (1, 3, 2):
            arrived(h, 3 + d)
            gather(h, 15 - d).start()

    def sibling_own_row(h):
        for slot in (7, 9, 10, 11):
            arrived(h, slot)

    def sibling_other_row(h):
        for slot in (8, 12, 13, 14):
            arrived(h, slot)

    def stage_a(h, y):
        return remote(send_a.at[h, y], recv_a.at[h, y], rs_send.at[h, y], rs_recv.at[h, y], sibling)

    def stage_c(h):
        return remote(send_c.at[h], recv_c.at[h], rs_send.at[h, 2], rs_recv.at[h, 2], across)

    def stage_b(h, j):
        return remote(send_b.at[h, zs[j]], recv_b.at[h, j], rs_send.at[h, 3 + j], rs_recv.at[h, 3 + j], around[j])

    def stage_x(h, j):
        return remote(send_x.at[h, :, xs[j]], recv_x.at[h, j], rs_send.at[h, 6 + j], rs_recv.at[h, 6 + j], beside[j])

    def stage_v(h):
        return remote(send_v.at[h], recv_v.at[h], rs_send.at[h, 9], rs_recv.at[h, 9], over)

    def stage_y(h):
        return remote(send_y.at[h], recv_y.at[h], rs_send.at[h, 10], rs_recv.at[h, 10], over)

    def stage_w(h, j):
        return remote(send_w.at[h, xs[j]], recv_w.at[h, j], rs_send.at[h, 11 + j], rs_recv.at[h, 11 + j], beside[j])

    def masks(cc, yy):
        for zz in range(4):
            build_masks((cc * 2 + yy) * 4 + zz, yy * 8 + zz * 2 + cc, src_blocks, table, words, mask_ref)

    pl.semaphore_wait(barrier, 9)
    send_own(0)
    gather(0, 0).start()
    send_own(None)
    gather(None, 0).start()
    for h in range(1, heads):
        gather(h, 0).start()
    words_copy.wait()
    table_copy.wait()
    masks(c, yh)
    relay_across(0)
    relay_across(None)
    masks(1 - c, yh)
    forward_own_row(0)
    forward_own_row(None)

    def exchange_rows(h):
        stage_a(h, 1 - yh).wait_recv()
        send_c[h] = (acc_a[1 - yh] + recv_a[h, 1 - yh].astype(F32)).astype(BF16)
        stage_c(h).start()

    def event_0(h):
        done = h - 1

        @pl.when((h >= 1) & (h <= heads))
        def _():
            for j in (0, 2, 1):
                stage_x(done, j).start()
            stage_v(done).start()

        @pl.when(h == 1)
        def _():
            exchange_rows(0)

        @pl.when(h + 1 < heads)
        def _():
            send_own(h + 1)
            relay_across(h + 1)

        @pl.when((h >= 1) & (h < heads))
        def _():
            forward_other_row(h)
            sibling_own_row(h)

    def event_1(h):
        done = h - 1

        @pl.when((h >= 1) & (h <= heads))
        def _():
            stage_a(done, yh).wait_recv()
            stage_c(done).wait_recv()
            total = acc_a[yh] + recv_a[done, yh].astype(F32) + recv_c[done].astype(F32)
            tot_b[...] = total
            send_b[done] = total.astype(BF16)
            for j in (0, 2, 1):
                stage_b(done, j).start()

        @pl.when(h >= 2)
        def _():
            cols = pl.ds(pl.multiple_of((h - 2) * hd, hd), hd)
            stage_y(h - 2).wait_recv()
            dk_ref[:, cols] = keep_k[lax.rem(h, 2), yl] + recv_y[h - 2].astype(F32)
            for j in range(3):
                stage_w(h - 2, j).wait_recv()
            dv_ref[:, cols] = (
                keep_v[lax.rem(h, 2), x]
                + recv_w[h - 2, 0].astype(F32)
                + recv_w[h - 2, 1].astype(F32)
                + recv_w[h - 2, 2].astype(F32)
            )

        @pl.when(h == 0)
        def _():
            sibling_own_row(None)
            sibling_own_row(0)

        @pl.when((h >= 1) & (h < heads))
        def _():
            sibling_other_row(h)

    def event_2(h):
        done = h - 1
        odd = lax.rem(h + 1, 2)

        @pl.when((h >= 1) & (h <= heads))
        def _():
            for j in range(3):
                stage_x(done, j).wait_recv()
            for y in range(2):
                keep_k[odd, y] = (
                    keep_k[odd, y]
                    + recv_x[done, 0, y].astype(F32)
                    + recv_x[done, 1, y].astype(F32)
                    + recv_x[done, 2, y].astype(F32)
                )
            send_y[done] = keep_k[odd, 1 - yl].astype(BF16)
            stage_y(done).start()
            stage_v(done).wait_recv()
            total = keep_v[odd] + recv_v[done].astype(F32)
            keep_v[odd] = total
            send_w[done] = total.astype(BF16)
            for j in (0, 2, 1):
                stage_w(done, j).start()

        @pl.when(h == 0)
        def _():
            forward_other_row(None)
            forward_other_row(0)
            masks(c, 1 - yh)

        @pl.when(h + 1 < heads)
        def _():
            forward_own_row(h + 1)

    def event_3(h):
        done = h - 1

        @pl.when((h >= 1) & (h <= heads))
        def _():
            cols = pl.ds(pl.multiple_of(done * hd, hd), hd)
            for j in range(3):
                stage_b(done, j).wait_recv()
            dq_ref[:, cols] = (
                tot_b[z]
                + recv_b[done, 0].astype(F32)
                + recv_b[done, 1].astype(F32)
                + recv_b[done, 2].astype(F32)
            )

        @pl.when(h == 0)
        def _():
            sibling_other_row(None)
            sibling_other_row(0)
            masks(1 - c, 1 - yh)

        @pl.when((h >= 1) & (h < heads))
        def _():
            exchange_rows(h)

    def compute(h, i):
        @pl.when((h == 0) & (i == 0))
        def _():
            for cp in kv_copies:
                cp.wait()

        @pl.when(i == 0)
        def _():
            kt[...] = k_all[h].T
            dk_acc[...] = jnp.zeros_like(dk_acc)
            dv_acc[...] = jnp.zeros_like(dv_acc)

        mine = jnp.where(h == 0, lax.rem(i, 2) == 0, i >= 2)
        own_row = jnp.where(h == 0, i < 2, (i == 0) | (i == 3))
        cc = jnp.where(mine, c, 1 - c)
        yy = jnp.where(own_row, yh, 1 - yh)
        at = pl.multiple_of((cc * 2 + yy) * rows, rows)
        q = qg[h, cc, yy, 0].reshape(rows, hd)
        g = qg[h, cc, yy, 1].reshape(rows, hd)
        norm = jnp.concatenate([nd[cc, yy, j, pl.ds(h, 1), :] for j in range(4)], axis=1) * LOG2E
        delta = jnp.concatenate([nd[cc, yy, j, pl.ds(heads + h, 1), :] for j in range(4)], axis=1)
        dqt = visit(scale, tile, q, g, norm, delta, k_all.at[h], v_all.at[h], kt[...], mask_ref, at,
                    dk_acc, dv_acc, sbuf)
        dq = dqt.T.reshape(4, 128, hd)

        @pl.when(mine)
        def _():
            acc_a[yy] = dq

        @pl.when(jnp.logical_not(mine))
        def _():
            send_a[h, yy] = dq.astype(BF16)
            stage_a(h, yy).start()

        @pl.when(i == 3)
        def _():
            send_x[h] = dk_acc[...].reshape(2, 4, 128, hd).astype(BF16)
            for y in range(2):
                keep_k[lax.rem(h, 2), y] = dk_acc[pl.ds(pl.multiple_of((y * 4 + x) * 128, 128), 128), :]
            send_v[h] = dv_acc[pl.ds(pl.multiple_of((1 - yl) * rows, rows), rows), :].reshape(4, 128, hd).astype(BF16)
            keep_v[lax.rem(h, 2)] = dv_acc[pl.ds(pl.multiple_of(yl * rows, rows), rows), :].reshape(4, 128, hd)

    def step(n, carry):
        h = n // 4
        i = lax.rem(n, 4)
        for k, event in enumerate((event_0, event_1, event_2, event_3)):
            @pl.when(i == k)
            def _(event=event):
                event(h)

        @pl.when(h < heads)
        def _():
            compute(h, i)

        return carry

    lax.fori_loop(0, heads * 4 + 6, step, 0)

    def drain(h, carry):
        for slot in range(15):
            gather(h, slot).wait_send()
        for y in range(2):
            stage_a(h, y).wait_send()
        for j in range(3):
            stage_b(h, j).wait_send()
            stage_x(h, j).wait_send()
            stage_w(h, j).wait_send()
        stage_c(h).wait_send()
        stage_v(h).wait_send()
        stage_y(h).wait_send()
        return carry

    for slot in range(15):
        gather(None, slot).wait_send()
    lax.fori_loop(0, heads, drain, 0)


def finish(scale, dq_ref, dk_ref, dv_ref, q_out, k_out, v_out):
    q_out[...] = (dq_ref[...] * scale).astype(BF16)
    k_out[...] = (dk_ref[...] * scale).astype(BF16)
    v_out[...] = dv_ref[...].astype(BF16)


def shards(queries, out_grad, outputs, log_norms, src_keys, src_values, block_list, block_count, mask_bits):
    heads = log_norms.shape[0]
    local, features = queries.shape
    hd = features // heads
    n_src = src_keys.shape[0]
    tile = 128
    vmem = pl.BlockSpec(memory_space=pltpu.VMEM)
    anyspace = pl.BlockSpec(memory_space=pl.ANY)
    wide = jax.ShapeDtypeStruct((local, features), F32)
    narrow = jax.ShapeDtypeStruct((local, features), BF16)
    sums = pl.pallas_call(
        functools.partial(core, heads, tile),
        out_shape=(wide, wide, wide),
        in_specs=[pl.BlockSpec(memory_space=pltpu.SMEM), vmem] + [anyspace] * 7,
        out_specs=(vmem, vmem, vmem),
        scratch_shapes=[
            pltpu.VMEM(mask_bits.shape, jnp.int32),
            pltpu.VMEM((8, 128), jnp.int32),
            pltpu.SMEM((8, 128), jnp.int32),
            pltpu.VMEM((n_src, 16 * 128), F32),
            pltpu.VMEM((heads, 2, 2, 2, 4, 128, hd), BF16),
            pltpu.VMEM((heads, 128, hd), BF16),
            pltpu.VMEM((2, 2, 4, 2 * heads, 128), F32),
            pltpu.VMEM((heads, n_src, hd), BF16),
            pltpu.VMEM((heads, n_src, hd), BF16),
            pltpu.VMEM((hd, n_src), BF16),
            pltpu.VMEM((n_src, 512), BF16),
            pltpu.VMEM((n_src, hd), F32),
            pltpu.VMEM((n_src, hd), F32),
            pltpu.VMEM((heads, 2, 4, 128, hd), BF16),
            pltpu.VMEM((heads, 2, 4, 128, hd), BF16),
            pltpu.VMEM((2, 4, 128, hd), F32),
            pltpu.VMEM((heads, 4, 128, hd), BF16),
            pltpu.VMEM((heads, 4, 128, hd), BF16),
            pltpu.VMEM((4, 128, hd), F32),
            pltpu.VMEM((heads, 4, 128, hd), BF16),
            pltpu.VMEM((heads, 3, 128, hd), BF16),
            pltpu.VMEM((heads, 2, 4, 128, hd), BF16),
            pltpu.VMEM((heads, 3, 2, 128, hd), BF16),
            pltpu.VMEM((2, 2, 128, hd), F32),
            pltpu.VMEM((heads, 4, 128, hd), BF16),
            pltpu.VMEM((heads, 4, 128, hd), BF16),
            pltpu.VMEM((2, 4, 128, hd), F32),
            pltpu.VMEM((heads, 128, hd), BF16),
            pltpu.VMEM((heads, 128, hd), BF16),
            pltpu.VMEM((heads, 4, 128, hd), BF16),
            pltpu.VMEM((heads, 3, 128, hd), BF16),
            pltpu.SemaphoreType.DMA((heads, 5)),
            pltpu.SemaphoreType.DMA((3,)),
            pltpu.SemaphoreType.DMA((heads, 15)),
            pltpu.SemaphoreType.DMA((heads, 15)),
            pltpu.SemaphoreType.DMA((15,)),
            pltpu.SemaphoreType.DMA((15,)),
            pltpu.SemaphoreType.DMA((heads, 14)),
            pltpu.SemaphoreType.DMA((heads, 14)),
        ],
        compiler_params=pltpu.CompilerParams(
            vmem_limit_bytes=48 << 20, collective_id=0, has_side_effects=True
        ),
        name="attention",
    )(block_count, block_list, mask_bits, queries, out_grad, outputs, log_norms, src_keys, src_values)
    return pl.pallas_call(
        functools.partial(finish, hd ** -0.5),
        out_shape=(narrow, narrow, narrow),
        in_specs=[vmem] * 3,
        out_specs=(vmem, vmem, vmem),
        name="finish",
    )(*sums)


def solution(mesh):
    rows = P(("src", "rep"), None)
    placed = (
        rows,
        rows,
        rows,
        P(None, ("src", "rep")),
        P("src", None),
        P("src", None),
        P("src", "rep", None, None),
        P("src", "rep"),
        P("src", "rep", None, None, None),
    )
    return jax.shard_map(shards, mesh=mesh, in_specs=placed, out_specs=(rows, rows, rows), check_vma=False)
```

time: 96.6 us -> 85.5 us (0.89)
  Pallas kernels: 87.9 us -> 74.9 us
  local copies, waits for them, and re-layouts: 4.65 us -> 8.94 us
  other arithmetic: 2.5 us -> 0 us
    pallas_call x1 -> x2, Pallas kernels: 87.9 us -> 74.9 us  [the longest x1 73 us: shards(): pl.pallas_call(functools.partial(core, heads, tile), out_shape=(wide, wid...]
    unnamed x11 -> x22, local copies, waits for them, and re-layouts: 4.5 us -> 8.94 us
    mul x1 -> x0, other arithmetic: 1 us -> none  [shards(): products = out_grad.astype(F32) * outputs.astype(F32)]
where the time goes in v3:
time: 85.5 us; the launch traced here: 85.2 us
  Pallas kernels  74.9 us (88%)
  local copies, waits for them, and re-layouts  8.94 us (10%)
  between operations  1.33 us (2%)
    pallas_call x1, Pallas kernels, shards(): pl.pallas_call(functools.partial(core, heads, tile), out_shape=(wide, wid...  73 us
    unnamed x22, local copies, waits for them, and re-layouts  8.94 us
    pallas_call x1, Pallas kernels, shards(): pl.pallas_call(functools.partial(finish, hd ** (-0.5)), out_shape=(narrow...  1.89 us

profile of v3, /device:TPU:0, one launch (start us, length us, event | category | flops | bytes accessed | tf_op | source)
XLA Modules:
  0.0 85.2 jit_solution(12311355904819708549)
XLA Ops:
  0.6 0.0 copy-start.10
  1.3 0.0 copy-done.10
  1.3 0.0 copy-start
  1.3 1.2 %copy-done = bf16[1024,512]{1,0:T(8,128)(2,1)S(1)} copy-done((bf16[1024,512]{1,0:T(8,128)(2,1)S(1)}, bf16[1024,512]{1,0:T(8,128)(2,1)}, u32[]{:S(2)}) %copy-start) | copy-done | bytes 1048600
  2.5 0.0 copy-start.1
  2.5 1.2 %copy-done.1 = bf16[1024,512]{1,0:T(8,128)(2,1)S(1)} copy-done((bf16[1024,512]{1,0:T(8,128)(2,1)S(1)}, bf16[1024,512]{1,0:T(8,128)(2,1)}, u32[]{:S(2)}) %copy-start.1) | copy-done | bytes 1048600
  3.8 0.0 copy-start.2
  3.8 1.0 %copy-done.2 = s32[1,1,96,8,128]{4,3,2,1,0:T(8,128)S(1)} copy-done((s32[1,1,96,8,128]{4,3,2,1,0:T(8,128)S(1)}, s32[1,1,96,8,128]{4,3,2,1,0:T(8,128)}, u32[]{:S(2)}) %copy-start.2) | copy-done | bytes 393240
  4.8 0.0 copy-start.6
  4.8 0.9 %copy-done.6 = bf16[128,512]{1,0:T(8,128)(2,1)S(1)} copy-done((bf16[128,512]{1,0:T(8,128)(2,1)S(1)}, bf16[128,512]{1,0:T(8,128)(2,1)}, u32[]{:S(2)}) %copy-start.6) | copy-done | bytes 131096
  5.7 0.0 copy-start.7
  5.7 0.9 %copy-done.7 = bf16[128,512]{1,0:T(8,128)(2,1)S(1)} copy-done((bf16[128,512]{1,0:T(8,128)(2,1)S(1)}, bf16[128,512]{1,0:T(8,128)(2,1)}, u32[]{:S(2)}) %copy-start.7) | copy-done | bytes 131096
  6.6 0.0 copy-start.8
  6.6 0.9 %copy-done.8 = bf16[128,512]{1,0:T(8,128)(2,1)S(1)} copy-done((bf16[128,512]{1,0:T(8,128)(2,1)S(1)}, bf16[128,512]{1,0:T(8,128)(2,1)}, u32[]{:S(2)}) %copy-start.8) | copy-done | bytes 131096
  7.5 0.0 copy-start.9
  7.5 0.7 copy-done.9
  8.2 73.0 %attention.1 = (f32[128,512]{1,0:T(8,128)S(1)}, f32[128,512]{1,0:T(8,128)S(1)}, f32[128,512]{1,0:T(8,128)S(1)}) custom-call(s32[1,1]{1,0:T(1,128)S(6)} %copy.12.count_ref, s32[1,1,2,96]{3,2,1,0:T(2,128)S(1)} %copy-done.10, s32[1,1,96,8,128]{4,3,2,1,0:T(8,128)S(1)} %copy-done.2, bf16[128,512]{1,0:T(8,128)(2,1)S(1)} %copy-done.6, ...), custom_call_target="tpu_custom_call" | custom-call | tf_op jit(solution)/shard_map/attention/pallas_call | solution.py:475
  81.2 0.0 copy-start.3
  81.2 0.7 copy-done.3
  81.9 0.0 copy-start.4
  81.9 0.7 copy-done.4
  82.6 0.0 copy-start.5
  82.6 0.7 copy-done.5
  83.3 1.9 %finish.1 = (bf16[128,512]{1,0:T(8,128)(2,1)}, bf16[128,512]{1,0:T(8,128)(2,1)}, bf16[128,512]{1,0:T(8,128)(2,1)}) custom-call(f32[128,512]{1,0:T(8,128)} %copy-done.3, f32[128,512]{1,0:T(8,128)} %copy-done.4, f32[128,512]{1,0:T(8,128)} %copy-done.5), custom_call_target="tpu_custom_call" | custom-call | tf_op jit(solution)/shard_map/finish/pallas_call | solution.py:526
Async XLA Ops:
  0.6 0.7 copy-start.10
  1.3 1.2 %copy-start = (bf16[1024,512]{1,0:T(8,128)(2,1)S(1)}, bf16[1024,512]{1,0:T(8,128)(2,1)}, u32[]{:S(2)}) copy-start(bf16[1024,512]{1,0:T(8,128)(2,1)} %k_hbm.1) | copy-start | bytes 3145732
  2.5 1.2 %copy-start.1 = (bf16[1024,512]{1,0:T(8,128)(2,1)S(1)}, bf16[1024,512]{1,0:T(8,128)(2,1)}, u32[]{:S(2)}) copy-start(bf16[1024,512]{1,0:T(8,128)(2,1)} %v_hbm.1) | copy-start | bytes 3145732
  3.8 1.0 %copy-start.2 = (s32[1,1,96,8,128]{4,3,2,1,0:T(8,128)S(1)}, s32[1,1,96,8,128]{4,3,2,1,0:T(8,128)}, u32[]{:S(2)}) copy-start(s32[1,1,96,8,128]{4,3,2,1,0:T(8,128)} %words_hbm.1) | copy-start | bytes 1179652
  4.8 0.9 %copy-start.6 = (bf16[128,512]{1,0:T(8,128)(2,1)S(1)}, bf16[128,512]{1,0:T(8,128)(2,1)}, u32[]{:S(2)}) copy-start(bf16[128,512]{1,0:T(8,128)(2,1)} %q_hbm.1) | copy-start | bytes 393220
  5.7 0.9 %copy-start.7 = (bf16[128,512]{1,0:T(8,128)(2,1)S(1)}, bf16[128,512]{1,0:T(8,128)(2,1)}, u32[]{:S(2)}) copy-start(bf16[128,512]{1,0:T(8,128)(2,1)} %g_hbm.1) | copy-start | bytes 393220
  6.6 0.9 %copy-start.8 = (bf16[128,512]{1,0:T(8,128)(2,1)S(1)}, bf16[128,512]{1,0:T(8,128)(2,1)}, u32[]{:S(2)}) copy-start(bf16[128,512]{1,0:T(8,128)(2,1)} %o_hbm.1) | copy-start | bytes 393220
  7.5 0.7 copy-start.9
  81.2 0.7 copy-start.3
  81.9 0.7 copy-start.4
  82.6 0.7 copy-start.5

commit v4 on v3

--- a/solution.py
+++ b/solution.py
@@ -285,6 +285,28 @@
             sibling_own_row(h)
 
     def event_1(h):
+        @pl.when(h >= 2)
+        def _():
+            cols = pl.ds(pl.multiple_of((h - 2) * hd, hd), hd)
+            for j in range(3):
+                stage_b((h - 2), j).wait_recv()
+            dq_ref[:, cols] = (
+                tot_b[z]
+                + recv_b[(h - 2), 0].astype(F32)
+                + recv_b[(h - 2), 1].astype(F32)
+                + recv_b[(h - 2), 2].astype(F32)
+            )
+
+        @pl.when(h == 0)
+        def _():
+            sibling_own_row(None)
+            sibling_own_row(0)
+
+        @pl.when((h >= 1) & (h < heads))
+        def _():
+            sibling_other_row(h)
+
+    def event_2(h):
         done = h - 1
 
         @pl.when((h >= 1) & (h <= heads))
@@ -313,15 +335,17 @@
 
         @pl.when(h == 0)
         def _():
-            sibling_own_row(None)
-            sibling_own_row(0)
-
-        @pl.when((h >= 1) & (h < heads))
-        def _():
-            sibling_other_row(h)
-
-    def event_2(h):
+            forward_other_row(None)
+            forward_other_row(0)
+            masks(c, 1 - yh)
+
+        @pl.when(h + 1 < heads)
+        def _():
+            forward_own_row(h + 1)
+
+    def event_3(h):
         done = h - 1
+
         odd = lax.rem(h + 1, 2)
 
         @pl.when((h >= 1) & (h <= heads))
@@ -346,31 +370,6 @@
 
         @pl.when(h == 0)
         def _():
-            forward_other_row(None)
-            forward_other_row(0)
-            masks(c, 1 - yh)
-
-        @pl.when(h + 1 < heads)
-        def _():
-            forward_own_row(h + 1)
-
-    def event_3(h):
-        done = h - 1
-
-        @pl.when((h >= 1) & (h <= heads))
-        def _():
-            cols = pl.ds(pl.multiple_of(done * hd, hd), hd)
-            for j in range(3):
-                stage_b(done, j).wait_recv()
-            dq_ref[:, cols] = (
-                tot_b[z]
-                + recv_b[done, 0].astype(F32)
-                + recv_b[done, 1].astype(F32)
-                + recv_b[done, 2].astype(F32)
-            )
-
-        @pl.when(h == 0)
-        def _():
             sibling_other_row(None)
             sibling_other_row(0)
             masks(1 - c, 1 - yh)
@@ -435,7 +434,7 @@
 
         return carry
 
-    lax.fori_loop(0, heads * 4 + 6, step, 0)
+    lax.fori_loop(0, heads * 4 + 7, step, 0)
 
     def drain(h, carry):
         for slot in range(15):
@@ -467,7 +466,7 @@
     local, features = queries.shape
     hd = features // heads
     n_src = src_keys.shape[0]
-    tile = 128
+    tile = 256
     vmem = pl.BlockSpec(memory_space=pltpu.VMEM)
     anyspace = pl.BlockSpec(memory_space=pl.ANY)
     wide = jax.ShapeDtypeStruct((local, features), F32)
@@ -519,7 +518,7 @@
             pltpu.SemaphoreType.DMA((heads, 14)),
         ],
         compiler_params=pltpu.CompilerParams(
-            vmem_limit_bytes=48 << 20, collective_id=0, has_side_effects=True
+            vmem_limit_bytes=67043328, collective_id=0, has_side_effects=True
         ),
         name="attention",
     )(block_count, block_list, mask_bits, queries, out_grad, outputs, log_norms, src_keys, src_values)

time: 85.5 us -> 69.1 us (0.81)
  local copies, waits for them, and re-layouts: 8.94 us -> 0 us
  Pallas kernels: 74.9 us -> 67.6 us
    unnamed x22 -> x0, local copies, waits for them, and re-layouts: 8.94 us -> none
    pallas_call x1, Pallas kernels: 73 us -> 65.7 us  [shards(): pl.pallas_call(functools.partial(core, heads, tile), out_shape=(wide, wid...]
where the time goes in v4:
time: 69.1 us; the launch traced here: 68.9 us
  Pallas kernels  67.6 us (98%)
  between operations  1.29 us (2%)
    pallas_call x1, Pallas kernels, shards(): pl.pallas_call(functools.partial(core, heads, tile), out_shape=(wide, wid...  65.7 us
    pallas_call x1, Pallas kernels, shards(): pl.pallas_call(functools.partial(finish, hd ** (-0.5)), out_shape=(narrow...  1.89 us

profile of v4, /device:TPU:0, one launch (start us, length us, event | category | flops | bytes accessed | tf_op | source)
XLA Modules:
  0.0 68.9 jit_solution(13902456382350462844)
XLA Ops:
  1.3 65.7 %attention.1 = (f32[128,512]{1,0:T(8,128)}, f32[128,512]{1,0:T(8,128)}, f32[128,512]{1,0:T(8,128)}) custom-call(s32[1,1]{1,0:T(1,128)S(6)} %copy.12.count_ref, s32[1,1,2,96]{3,2,1,0:T(2,128)} %list_ref.1, s32[1,1,96,8,128]{4,3,2,1,0:T(8,128)} %words_hbm.1, bf16[128,512]{1,0:T(8,128)(2,1)} %q_hbm.1, bf16[128,512]{1,0:T(8,128)(2,1)} %g_hbm.1, ...), custom_call_target="tpu_custom_call" | custom-call | tf_op jit(solution)/shard_map/attention/pallas_call | solution.py:474
  67.0 1.9 %finish.1 = (bf16[128,512]{1,0:T(8,128)(2,1)}, bf16[128,512]{1,0:T(8,128)(2,1)}, bf16[128,512]{1,0:T(8,128)(2,1)}) custom-call(f32[128,512]{1,0:T(8,128)} %get-tuple-element.6.dq_ref, f32[128,512]{1,0:T(8,128)} %get-tuple-element.7.dk_ref, f32[128,512]{1,0:T(8,128)} %get-tuple-element.8.dv_ref), custom_call_target="tpu_custom_call" | custom-call | tf_op jit(solution)/shard_map/finish/pallas_call | solution.py:525

commit v5 on v4

--- a/solution.py
+++ b/solution.py
@@ -82,7 +82,7 @@
          dq_ref, dk_ref, dv_ref,
          words, slots, table, mask_ref, qg, o_all, nd, k_all, v_all, kt, sbuf, dk_acc, dv_acc,
          send_a, recv_a, acc_a, send_c, recv_c, tot_b, send_b, recv_b,
-         send_x, recv_x, keep_k, send_v, recv_v, keep_v, send_y, recv_y, send_w, recv_w,
+         send_x, recv_x, keep, send_y, recv_y, recv_v, tot_w, send_w, recv_w,
          local_sem, extra_sem, ag_send, ag_recv, nd_send, nd_recv, rs_send, rs_recv):
     hd = kt.shape[0]
     n_src = kt.shape[1]
@@ -135,13 +135,6 @@
     table_copy = pltpu.make_async_copy(slots, table, extra_sem.at[2])
     table_copy.start()
 
-    norm_copy.wait()
-    for cp in mine_copies:
-        cp.wait()
-    for h in range(heads):
-        product = qg[h, c, yh, 1, z].astype(F32) * o_all[h].astype(F32)
-        nd[c, yh, z, heads + h : heads + h + 1, :] = jnp.sum(product.T, axis=0, keepdims=True)
-
     def remote(a, b, s, r, peer):
         return pltpu.make_async_remote_copy(
             src_ref=a, dst_ref=b, send_sem=s, recv_sem=r, device_id=peer, device_id_type=MESH
@@ -207,6 +200,39 @@
             arrived(h, 3 + d)
             gather(h, 15 - d).start()
 
+    def half(h, yy, zz, part, slot, peer):
+        ref = qg.at[h, c, yy, part, zz]
+        return remote(ref, ref, ag_send.at[h, slot], ag_recv.at[h, slot], peer)
+
+    def ring_own(h):
+        for slot in (1, 3, 7):
+            gather(h, slot).start()
+
+    def ring_across(h):
+        arrived(h, 0)
+        for slot in (4, 6, 8):
+            gather(h, slot).start()
+
+    def ring_halves(h):
+        return [
+            (1, 11, half(h, yh, zs[2], 0, 2, around[0])),
+            (3, 9, half(h, yh, zs[0], 1, 15, around[2])),
+            (4, 14, half(h, 1 - yh, zs[2], 0, 5, around[0])),
+            (6, 12, half(h, 1 - yh, zs[0], 1, 16, around[2])),
+        ]
+
+    def ring_forward(h):
+        for slot, core_slot, onward in ring_halves(h):
+            arrived(h, slot)
+            onward.start()
+            gather(h, core_slot).start()
+
+    def ring_finish(h):
+        for yy, slots_, core_slot in ((yh, (2, 15), 10), (1 - yh, (5, 16), 13)):
+            for part in range(2):
+                half(h, yy, zs[1], part, slots_[part], sibling).wait_recv()
+            gather(h, core_slot).start()
+
     def sibling_own_row(h):
         for slot in (7, 9, 10, 11):
             arrived(h, slot)
@@ -225,24 +251,41 @@
         return remote(send_b.at[h, zs[j]], recv_b.at[h, j], rs_send.at[h, 3 + j], rs_recv.at[h, 3 + j], around[j])
 
     def stage_x(h, j):
-        return remote(send_x.at[h, :, xs[j]], recv_x.at[h, j], rs_send.at[h, 6 + j], rs_recv.at[h, 6 + j], beside[j])
-
-    def stage_v(h):
-        return remote(send_v.at[h], recv_v.at[h], rs_send.at[h, 9], rs_recv.at[h, 9], over)
+        return remote(send_x.at[h, :, :, xs[j]], recv_x.at[h, j], rs_send.at[h, 6 + j], rs_recv.at[h, 6 + j], beside[j])
 
     def stage_y(h):
-        return remote(send_y.at[h], recv_y.at[h], rs_send.at[h, 10], rs_recv.at[h, 10], over)
-
-    def stage_w(h, j):
-        return remote(send_w.at[h, xs[j]], recv_w.at[h, j], rs_send.at[h, 11 + j], rs_recv.at[h, 11 + j], beside[j])
+        return remote(send_y.at[h], recv_y.at[h], rs_send.at[h, 9], rs_recv.at[h, 9], over)
+
+    last = heads - 1
+
+    def last_x(j):
+        return remote(send_x.at[last, 0, :, xs[j]], recv_x.at[last, j, 0], rs_send.at[last, 6 + j],
+                      rs_recv.at[last, 6 + j], beside[j])
+
+    def last_y():
+        return remote(send_y.at[last, 0], recv_y.at[last, 0], rs_send.at[last, 9], rs_recv.at[last, 9], over)
+
+    def last_v():
+        return remote(send_x.at[last, 1, 1 - yl], recv_v, rs_send.at[last, 10], rs_recv.at[last, 10], over)
+
+    def last_w(j):
+        return remote(send_w.at[xs[j]], recv_w.at[j], rs_send.at[last, 11 + j], rs_recv.at[last, 11 + j], beside[j])
 
     def masks(cc, yy):
         for zz in range(4):
             build_masks((cc * 2 + yy) * 4 + zz, yy * 8 + zz * 2 + cc, src_blocks, table, words, mask_ref)
 
+    for cp in mine_copies[:2]:
+        cp.wait()
     pl.semaphore_wait(barrier, 9)
     send_own(0)
     gather(0, 0).start()
+    norm_copy.wait()
+    for cp in mine_copies[2:]:
+        cp.wait()
+    for h in range(heads):
+        product = qg[h, c, yh, 1, z].astype(F32) * o_all[h].astype(F32)
+        nd[c, yh, z, heads + h : heads + h + 1, :] = jnp.sum(product.T, axis=0, keepdims=True)
     send_own(None)
     gather(None, 0).start()
     for h in range(1, heads):
@@ -264,25 +307,48 @@
     def event_0(h):
         done = h - 1
 
-        @pl.when((h >= 1) & (h <= heads))
+        @pl.when((h >= 1) & (h < heads))
         def _():
             for j in (0, 2, 1):
                 stage_x(done, j).start()
-            stage_v(done).start()
+
+        @pl.when(h == heads)
+        def _():
+            last_v().start()
+            for j in (0, 2, 1):
+                last_x(j).start()
 
         @pl.when(h == 1)
         def _():
             exchange_rows(0)
 
-        @pl.when(h + 1 < heads)
-        def _():
-            send_own(h + 1)
-            relay_across(h + 1)
+        @pl.when(h == 0)
+        def _():
+            send_own(1)
+            relay_across(1)
+
+        @pl.when(h == 1)
+        def _():
+            forward_other_row(1)
 
         @pl.when((h >= 1) & (h < heads))
         def _():
-            forward_other_row(h)
             sibling_own_row(h)
+
+        @pl.when((h >= 2) & (h <= heads))
+        def _():
+            for j in range(3):
+                stage_x(h - 2, j).wait_recv()
+            for a in range(2):
+                for y in range(2):
+                    keep[lax.rem(h, 2), a, y] = (
+                        keep[lax.rem(h, 2), a, y]
+                        + recv_x[h - 2, 0, a, y].astype(F32)
+                        + recv_x[h - 2, 1, a, y].astype(F32)
+                        + recv_x[h - 2, 2, a, y].astype(F32)
+                    )
+                send_y[h - 2, a] = keep[lax.rem(h, 2), a, 1 - yl].astype(BF16)
+            stage_y(h - 2).start()
 
     def event_1(h):
         @pl.when(h >= 2)
@@ -319,18 +385,15 @@
             for j in (0, 2, 1):
                 stage_b(done, j).start()
 
-        @pl.when(h >= 2)
-        def _():
-            cols = pl.ds(pl.multiple_of((h - 2) * hd, hd), hd)
-            stage_y(h - 2).wait_recv()
-            dk_ref[:, cols] = keep_k[lax.rem(h, 2), yl] + recv_y[h - 2].astype(F32)
+        @pl.when(h == heads + 1)
+        def _():
+            cols = pl.ds(last * hd, hd)
+            last_y().wait_recv()
+            dk_ref[:, cols] = keep[last % 2, 0, yl] + recv_y[last, 0].astype(F32)
             for j in range(3):
-                stage_w(h - 2, j).wait_recv()
+                last_w(j).wait_recv()
             dv_ref[:, cols] = (
-                keep_v[lax.rem(h, 2), x]
-                + recv_w[h - 2, 0].astype(F32)
-                + recv_w[h - 2, 1].astype(F32)
-                + recv_w[h - 2, 2].astype(F32)
+                tot_w[x] + recv_w[0].astype(F32) + recv_w[1].astype(F32) + recv_w[2].astype(F32)
             )
 
         @pl.when(h == 0)
@@ -343,30 +406,42 @@
         def _():
             forward_own_row(h + 1)
 
+        @pl.when(h + 2 < heads)
+        def _():
+            send_own(h + 2)
+            relay_across(h + 2)
+
     def event_3(h):
         done = h - 1
 
         odd = lax.rem(h + 1, 2)
 
-        @pl.when((h >= 1) & (h <= heads))
-        def _():
+        @pl.when(h == heads)
+        def _():
+            last_v().wait_recv()
+            total = dv_acc[pl.ds(pl.multiple_of(yl * rows, rows), rows), :].reshape(4, 128, hd) + recv_v[...].astype(F32)
+            tot_w[...] = total
+            send_w[...] = total.astype(BF16)
+            for j in (0, 2, 1):
+                last_w(j).start()
             for j in range(3):
-                stage_x(done, j).wait_recv()
+                last_x(j).wait_recv()
             for y in range(2):
-                keep_k[odd, y] = (
-                    keep_k[odd, y]
-                    + recv_x[done, 0, y].astype(F32)
-                    + recv_x[done, 1, y].astype(F32)
-                    + recv_x[done, 2, y].astype(F32)
+                keep[odd, 0, y] = (
+                    keep[odd, 0, y]
+                    + recv_x[last, 0, 0, y].astype(F32)
+                    + recv_x[last, 1, 0, y].astype(F32)
+                    + recv_x[last, 2, 0, y].astype(F32)
                 )
-            send_y[done] = keep_k[odd, 1 - yl].astype(BF16)
-            stage_y(done).start()
-            stage_v(done).wait_recv()
-            total = keep_v[odd] + recv_v[done].astype(F32)
-            keep_v[odd] = total
-            send_w[done] = total.astype(BF16)
-            for j in (0, 2, 1):
-                stage_w(done, j).start()
+            send_y[last, 0] = keep[odd, 0, 1 - yl].astype(BF16)
+            last_y().start()
+
+        @pl.when((h >= 2) & (h <= heads))
+        def _():
+            cols = pl.ds(pl.multiple_of((h - 2) * hd, hd), hd)
+            stage_y(h - 2).wait_recv()
+            dk_ref[:, cols] = keep[lax.rem(h, 2), 0, yl] + recv_y[h - 2, 0].astype(F32)
+            dv_ref[:, cols] = keep[lax.rem(h, 2), 1, yl] + recv_y[h - 2, 1].astype(F32)
 
         @pl.when(h == 0)
         def _():
@@ -377,6 +452,10 @@
         @pl.when((h >= 1) & (h < heads))
         def _():
             exchange_rows(h)
+
+        @pl.when((h >= 1) & (h + 1 < heads))
+        def _():
+            forward_other_row(h + 1)
 
     def compute(h, i):
         @pl.when((h == 0) & (i == 0))
@@ -414,11 +493,10 @@
 
         @pl.when(i == 3)
         def _():
-            send_x[h] = dk_acc[...].reshape(2, 4, 128, hd).astype(BF16)
-            for y in range(2):
-                keep_k[lax.rem(h, 2), y] = dk_acc[pl.ds(pl.multiple_of((y * 4 + x) * 128, 128), 128), :]
-            send_v[h] = dv_acc[pl.ds(pl.multiple_of((1 - yl) * rows, rows), rows), :].reshape(4, 128, hd).astype(BF16)
-            keep_v[lax.rem(h, 2)] = dv_acc[pl.ds(pl.multiple_of(yl * rows, rows), rows), :].reshape(4, 128, hd)
+            for a, acc in enumerate((dk_acc, dv_acc)):
+                send_x[h, a] = acc[...].reshape(2, 4, 128, hd).astype(BF16)
+                for y in range(2):
+                    keep[lax.rem(h, 2), a, y] = acc[pl.ds(pl.multiple_of((y * 4 + x) * 128, 128), 128), :]
 
     def step(n, carry):
         h = n // 4
@@ -436,23 +514,36 @@
 
     lax.fori_loop(0, heads * 4 + 7, step, 0)
 
-    def drain(h, carry):
-        for slot in range(15):
-            gather(h, slot).wait_send()
+    def drain_reduce(h):
         for y in range(2):
             stage_a(h, y).wait_send()
         for j in range(3):
             stage_b(h, j).wait_send()
+        stage_c(h).wait_send()
+
+    def drain_gather(h, carry):
+        for slot in range(15):
+            gather(h, slot).wait_send()
+        return carry
+
+    def drain(h, carry):
+        drain_reduce(h)
+        for j in range(3):
             stage_x(h, j).wait_send()
-            stage_w(h, j).wait_send()
-        stage_c(h).wait_send()
-        stage_v(h).wait_send()
         stage_y(h).wait_send()
         return carry
 
     for slot in range(15):
         gather(None, slot).wait_send()
-    lax.fori_loop(0, heads, drain, 0)
+        gather(0, slot).wait_send()
+    lax.fori_loop(1, heads, drain_gather, 0)
+    lax.fori_loop(0, last, drain, 0)
+    drain_reduce(last)
+    last_v().wait_send()
+    last_y().wait_send()
+    for j in range(3):
+        last_x(j).wait_send()
+        last_w(j).wait_send()
 
 
 def finish(scale, dq_ref, dk_ref, dv_ref, q_out, k_out, v_out):
@@ -498,20 +589,19 @@
             pltpu.VMEM((4, 128, hd), F32),
             pltpu.VMEM((heads, 4, 128, hd), BF16),
             pltpu.VMEM((heads, 3, 128, hd), BF16),
-            pltpu.VMEM((heads, 2, 4, 128, hd), BF16),
-            pltpu.VMEM((heads, 3, 2, 128, hd), BF16),
-            pltpu.VMEM((2, 2, 128, hd), F32),
-            pltpu.VMEM((heads, 4, 128, hd), BF16),
-            pltpu.VMEM((heads, 4, 128, hd), BF16),
-            pltpu.VMEM((2, 4, 128, hd), F32),
-            pltpu.VMEM((heads, 128, hd), BF16),
-            pltpu.VMEM((heads, 128, hd), BF16),
-            pltpu.VMEM((heads, 4, 128, hd), BF16),
-            pltpu.VMEM((heads, 3, 128, hd), BF16),
+            pltpu.VMEM((heads, 2, 2, 4, 128, hd), BF16),
+            pltpu.VMEM((heads, 3, 2, 2, 128, hd), BF16),
+            pltpu.VMEM((2, 2, 2, 128, hd), F32),
+            pltpu.VMEM((heads, 2, 128, hd), BF16),
+            pltpu.VMEM((heads, 2, 128, hd), BF16),
+            pltpu.VMEM((4, 128, hd), BF16),
+            pltpu.VMEM((4, 128, hd), F32),
+            pltpu.VMEM((4, 128, hd), BF16),
+            pltpu.VMEM((3, 128, hd), BF16),
             pltpu.SemaphoreType.DMA((heads, 5)),
             pltpu.SemaphoreType.DMA((3,)),
-            pltpu.SemaphoreType.DMA((heads, 15)),
-            pltpu.SemaphoreType.DMA((heads, 15)),
+            pltpu.SemaphoreType.DMA((heads, 17)),
+            pltpu.SemaphoreType.DMA((heads, 17)),
             pltpu.SemaphoreType.DMA((15,)),
             pltpu.SemaphoreType.DMA((15,)),
             pltpu.SemaphoreType.DMA((heads, 14)),

time: 69.1 us -> 66.7 us (0.965)
  Pallas kernels: 67.6 us -> 65.3 us
    pallas_call x1, Pallas kernels: 65.7 us -> 63.4 us  [shards(): pl.pallas_call(functools.partial(core, heads, tile), out_shape=(wide, wid...]
where the time goes in v5:
time: 66.7 us; the launch traced here: 66.6 us
  Pallas kernels  65.3 us (98%)
  between operations  1.29 us (2%)
    pallas_call x1, Pallas kernels, shards(): pl.pallas_call(functools.partial(core, heads, tile), out_shape=(wide, wid...  63.4 us
    pallas_call x1, Pallas kernels, shards(): pl.pallas_call(functools.partial(finish, hd ** (-0.5)), out_shape=(narrow...  1.89 us

profile of v5, /device:TPU:0, one launch (start us, length us, event | category | flops | bytes accessed | tf_op | source)
XLA Modules:
  0.0 66.6 jit_solution(17906291963617342321)
XLA Ops:
  1.3 63.4 %attention.1 = (f32[128,512]{1,0:T(8,128)}, f32[128,512]{1,0:T(8,128)}, f32[128,512]{1,0:T(8,128)}) custom-call(s32[1,1]{1,0:T(1,128)S(6)} %copy.12.count_ref, s32[1,1,2,96]{3,2,1,0:T(2,128)} %list_ref.1, s32[1,1,96,8,128]{4,3,2,1,0:T(8,128)} %words_hbm.1, bf16[128,512]{1,0:T(8,128)(2,1)} %q_hbm.1, bf16[128,512]{1,0:T(8,128)(2,1)} %g_hbm.1, ...), custom_call_target="tpu_custom_call" | custom-call | tf_op jit(solution)/shard_map/attention/pallas_call | solution.py:565
  64.7 1.9 %finish.1 = (bf16[128,512]{1,0:T(8,128)(2,1)}, bf16[128,512]{1,0:T(8,128)(2,1)}, bf16[128,512]{1,0:T(8,128)(2,1)}) custom-call(f32[128,512]{1,0:T(8,128)} %get-tuple-element.6.dq_ref, f32[128,512]{1,0:T(8,128)} %get-tuple-element.7.dk_ref, f32[128,512]{1,0:T(8,128)} %get-tuple-element.8.dv_ref), custom_call_target="tpu_custom_call" | custom-call | tf_op jit(solution)/shard_map/finish/pallas_call | solution.py:615

commit v6 on v5

--- a/solution.py
+++ b/solution.py
@@ -79,11 +79,12 @@
 
 
 def core(heads, tile, count_ref, list_ref, words_hbm, q_hbm, g_hbm, o_hbm, norm_hbm, k_hbm, v_hbm,
-         dq_ref, dk_ref, dv_ref,
+         out_ref,
          words, slots, table, mask_ref, qg, o_all, nd, k_all, v_all, kt, sbuf, dk_acc, dv_acc,
          send_a, recv_a, acc_a, send_c, recv_c, tot_b, send_b, recv_b,
          send_x, recv_x, keep, send_y, recv_y, recv_v, tot_w, send_w, recv_w,
          local_sem, extra_sem, ag_send, ag_recv, nd_send, nd_recv, rs_send, rs_recv):
+    dq_ref, dk_ref, dv_ref = out_ref.at[0], out_ref.at[1], out_ref.at[2]
     hd = kt.shape[0]
     n_src = kt.shape[1]
     src_blocks = n_src // 128
@@ -296,6 +297,8 @@
     relay_across(0)
     relay_across(None)
     masks(1 - c, yh)
+    masks(c, 1 - yh)
+    masks(1 - c, 1 - yh)
     forward_own_row(0)
     forward_own_row(None)
 
@@ -356,12 +359,13 @@
             cols = pl.ds(pl.multiple_of((h - 2) * hd, hd), hd)
             for j in range(3):
                 stage_b((h - 2), j).wait_recv()
-            dq_ref[:, cols] = (
+            total = (
                 tot_b[z]
                 + recv_b[(h - 2), 0].astype(F32)
                 + recv_b[(h - 2), 1].astype(F32)
                 + recv_b[(h - 2), 2].astype(F32)
             )
+            dq_ref[:, cols] = (total * scale).T.astype(BF16)
 
         @pl.when(h == 0)
         def _():
@@ -389,18 +393,17 @@
         def _():
             cols = pl.ds(last * hd, hd)
             last_y().wait_recv()
-            dk_ref[:, cols] = keep[last % 2, 0, yl] + recv_y[last, 0].astype(F32)
+            dk_ref[:, cols] = ((keep[last % 2, 0, yl] + recv_y[last, 0].astype(F32)) * scale).astype(BF16)
             for j in range(3):
                 last_w(j).wait_recv()
             dv_ref[:, cols] = (
                 tot_w[x] + recv_w[0].astype(F32) + recv_w[1].astype(F32) + recv_w[2].astype(F32)
-            )
+            ).astype(BF16)
 
         @pl.when(h == 0)
         def _():
             forward_other_row(None)
             forward_other_row(0)
-            masks(c, 1 - yh)
 
         @pl.when(h + 1 < heads)
         def _():
@@ -440,14 +443,13 @@
         def _():
             cols = pl.ds(pl.multiple_of((h - 2) * hd, hd), hd)
             stage_y(h - 2).wait_recv()
-            dk_ref[:, cols] = keep[lax.rem(h, 2), 0, yl] + recv_y[h - 2, 0].astype(F32)
-            dv_ref[:, cols] = keep[lax.rem(h, 2), 1, yl] + recv_y[h - 2, 1].astype(F32)
+            dk_ref[:, cols] = ((keep[lax.rem(h, 2), 0, yl] + recv_y[h - 2, 0].astype(F32)) * scale).astype(BF16)
+            dv_ref[:, cols] = (keep[lax.rem(h, 2), 1, yl] + recv_y[h - 2, 1].astype(F32)).astype(BF16)
 
         @pl.when(h == 0)
         def _():
             sibling_other_row(None)
             sibling_other_row(0)
-            masks(1 - c, 1 - yh)
 
         @pl.when((h >= 1) & (h < heads))
         def _():
@@ -480,15 +482,16 @@
         delta = jnp.concatenate([nd[cc, yy, j, pl.ds(heads + h, 1), :] for j in range(4)], axis=1)
         dqt = visit(scale, tile, q, g, norm, delta, k_all.at[h], v_all.at[h], kt[...], mask_ref, at,
                     dk_acc, dv_acc, sbuf)
-        dq = dqt.T.reshape(4, 128, hd)
 
         @pl.when(mine)
         def _():
-            acc_a[yy] = dq
+            for j in range(4):
+                acc_a[yy, j] = dqt[:, j * 128 : (j + 1) * 128]
 
         @pl.when(jnp.logical_not(mine))
         def _():
-            send_a[h, yy] = dq.astype(BF16)
+            for j in range(4):
+                send_a[h, yy, j] = dqt[:, j * 128 : (j + 1) * 128].astype(BF16)
             stage_a(h, yy).start()
 
         @pl.when(i == 3)
@@ -546,10 +549,9 @@
         last_w(j).wait_send()
 
 
-def finish(scale, dq_ref, dk_ref, dv_ref, q_out, k_out, v_out):
-    q_out[...] = (dq_ref[...] * scale).astype(BF16)
-    k_out[...] = (dk_ref[...] * scale).astype(BF16)
-    v_out[...] = dv_ref[...].astype(BF16)
+def finish(sums_ref, q_out, k_out, v_out):
+    for i, out in enumerate((q_out, k_out, v_out)):
+        out[...] = sums_ref[i]
 
 
 def shards(queries, out_grad, outputs, log_norms, src_keys, src_values, block_list, block_count, mask_bits):
@@ -560,13 +562,12 @@
     tile = 256
     vmem = pl.BlockSpec(memory_space=pltpu.VMEM)
     anyspace = pl.BlockSpec(memory_space=pl.ANY)
-    wide = jax.ShapeDtypeStruct((local, features), F32)
     narrow = jax.ShapeDtypeStruct((local, features), BF16)
     sums = pl.pallas_call(
         functools.partial(core, heads, tile),
-        out_shape=(wide, wide, wide),
+        out_shape=jax.ShapeDtypeStruct((3, local, features), BF16),
         in_specs=[pl.BlockSpec(memory_space=pltpu.SMEM), vmem] + [anyspace] * 7,
-        out_specs=(vmem, vmem, vmem),
+        out_specs=vmem,
         scratch_shapes=[
             pltpu.VMEM(mask_bits.shape, jnp.int32),
             pltpu.VMEM((8, 128), jnp.int32),
@@ -581,14 +582,14 @@
             pltpu.VMEM((n_src, 512), BF16),
             pltpu.VMEM((n_src, hd), F32),
             pltpu.VMEM((n_src, hd), F32),
-            pltpu.VMEM((heads, 2, 4, 128, hd), BF16),
-            pltpu.VMEM((heads, 2, 4, 128, hd), BF16),
-            pltpu.VMEM((2, 4, 128, hd), F32),
-            pltpu.VMEM((heads, 4, 128, hd), BF16),
-            pltpu.VMEM((heads, 4, 128, hd), BF16),
-            pltpu.VMEM((4, 128, hd), F32),
-            pltpu.VMEM((heads, 4, 128, hd), BF16),
-            pltpu.VMEM((heads, 3, 128, hd), BF16),
+            pltpu.VMEM((heads, 2, 4, hd, 128), BF16),
+            pltpu.VMEM((heads, 2, 4, hd, 128), BF16),
+            pltpu.VMEM((2, 4, hd, 128), F32),
+            pltpu.VMEM((heads, 4, hd, 128), BF16),
+            pltpu.VMEM((heads, 4, hd, 128), BF16),
+            pltpu.VMEM((4, hd, 128), F32),
+            pltpu.VMEM((heads, 4, hd, 128), BF16),
+            pltpu.VMEM((heads, 3, hd, 128), BF16),
             pltpu.VMEM((heads, 2, 2, 4, 128, hd), BF16),
             pltpu.VMEM((heads, 3, 2, 2, 128, hd), BF16),
             pltpu.VMEM((2, 2, 2, 128, hd), F32),
@@ -613,12 +614,12 @@
         name="attention",
     )(block_count, block_list, mask_bits, queries, out_grad, outputs, log_norms, src_keys, src_values)
     return pl.pallas_call(
-        functools.partial(finish, hd ** -0.5),
+        finish,
         out_shape=(narrow, narrow, narrow),
-        in_specs=[vmem] * 3,
+        in_specs=[vmem],
         out_specs=(vmem, vmem, vmem),
         name="finish",
-    )(*sums)
+    )(sums)
 
 
 def solution(mesh):

time: 66.7 us -> 65.7 us (0.985)
  Pallas kernels: 65.3 us -> 64.2 us
    pallas_call x2, Pallas kernels: 65.3 us -> 64.2 us  [the longest x1 62.4 us: shards(): pl.pallas_call(functools.partial(core, heads, tile), out_shape=jax.ShapeD...]
where the time goes in v6:
time: 65.7 us; the launch traced here: 65.5 us
  Pallas kernels  64.2 us (98%)
  between operations  1.29 us (2%)
    pallas_call x1, Pallas kernels, shards(): pl.pallas_call(functools.partial(core, heads, tile), out_shape=jax.ShapeD...  62.4 us
    pallas_call x1, Pallas kernels, shards(): pl.pallas_call(finish, out_shape=(narrow, narrow, narrow), in_specs=[vmem...  1.75 us

profile of v6, /device:TPU:0, one launch (start us, length us, event | category | flops | bytes accessed | tf_op | source)
XLA Modules:
  0.0 65.5 jit_solution(3208231042400952857)
XLA Ops:
  1.3 62.4 %attention.1.sums_ref = bf16[3,128,512]{2,1,0:T(8,128)(2,1)} custom-call(s32[1,1]{1,0:T(1,128)S(6)} %copy.12.count_ref, s32[1,1,2,96]{3,2,1,0:T(2,128)} %list_ref.1, s32[1,1,96,8,128]{4,3,2,1,0:T(8,128)} %words_hbm.1, bf16[128,512]{1,0:T(8,128)(2,1)} %q_hbm.1, bf16[128,512]{1,0:T(8,128)(2,1)} %g_hbm.1, bf16[128,512]{1,0:T(8,128)(2,1)} %o_hbm.1, ...), custom_call_target="tpu_custom_call" | custom-call | tf_op jit(solution)/shard_map/attention/pallas_call | solution.py:566
  63.7 1.7 %finish.1 = (bf16[128,512]{1,0:T(8,128)(2,1)}, bf16[128,512]{1,0:T(8,128)(2,1)}, bf16[128,512]{1,0:T(8,128)(2,1)}) custom-call(bf16[3,128,512]{2,1,0:T(8,128)(2,1)} %attention.1.sums_ref), custom_call_target="tpu_custom_call" | custom-call | tf_op jit(solution)/shard_map/finish/pallas_call | solution.py:616

commit v7 on v6

--- a/solution.py
+++ b/solution.py
@@ -43,7 +43,7 @@
         [jnp.bitwise_and(words, 255), jnp.bitwise_and(jnp.right_shift(words, 8), 255)], axis=0
     )
     wide = tn_dot(halves.astype(F32).astype(BF16), spread).astype(jnp.int32)
-    picked = jnp.where(jnp.bitwise_and(wide, bit) != 0, 1.0, 0.0)
+    picked = jnp.where(jnp.bitwise_and(wide, bit) != 0, 0.0, -1e30)
     mask_ref[:, pl.ds(pl.multiple_of(u * 128, 128), 128)] = picked
 
 
@@ -53,8 +53,7 @@
     for c in range(n_src // tile):
         cs = pl.ds(c * tile, tile)
         s = nt_dot(k_ref[cs, :], q)
-        e = jnp.exp2(s * (scale * LOG2E) - norm)
-        p = e * mask_ref[cs, pl.ds(at, rows)]
+        p = jnp.exp2((s * (scale * LOG2E) - norm) + mask_ref[cs, pl.ds(at, rows)])
         d = nt_dot(v_ref[cs, :], g)
         ds = p * (d - delta)
         p_low = p.astype(BF16)

time: 65.7 us -> 65.7 us (level)
  no operation moved by 1% of the time
where the time goes in v7:
time: 65.7 us; the launch traced here: 65.5 us
  Pallas kernels  64.2 us (98%)
  between operations  1.29 us (2%)
    pallas_call x1, Pallas kernels, shards(): pl.pallas_call(functools.partial(core, heads, tile), out_shape=jax.ShapeD...  62.4 us
    pallas_call x1, Pallas kernels, shards(): pl.pallas_call(finish, out_shape=(narrow, narrow, narrow), in_specs=[vmem...  1.75 us

profile of v7, /device:TPU:0, one launch (start us, length us, event | category | flops | bytes accessed | tf_op | source)
XLA Modules:
  0.0 65.5 jit_solution(8949544944371022115)
XLA Ops:
  1.3 62.4 %attention.1.sums_ref = bf16[3,128,512]{2,1,0:T(8,128)(2,1)} custom-call(s32[1,1]{1,0:T(1,128)S(6)} %copy.12.count_ref, s32[1,1,2,96]{3,2,1,0:T(2,128)} %list_ref.1, s32[1,1,96,8,128]{4,3,2,1,0:T(8,128)} %words_hbm.1, bf16[128,512]{1,0:T(8,128)(2,1)} %q_hbm.1, bf16[128,512]{1,0:T(8,128)(2,1)} %g_hbm.1, bf16[128,512]{1,0:T(8,128)(2,1)} %o_hbm.1, ...), custom_call_target="tpu_custom_call" | custom-call | tf_op jit(solution)/shard_map/attention/pallas_call | solution.py:565
  63.7 1.7 %finish.1 = (bf16[128,512]{1,0:T(8,128)(2,1)}, bf16[128,512]{1,0:T(8,128)(2,1)}, bf16[128,512]{1,0:T(8,128)(2,1)}) custom-call(bf16[3,128,512]{2,1,0:T(8,128)(2,1)} %attention.1.sums_ref), custom_call_target="tpu_custom_call" | custom-call | tf_op jit(solution)/shard_map/finish/pallas_call | solution.py:615

commit v8 on v7

--- a/solution.py
+++ b/solution.py
@@ -182,12 +182,12 @@
         gather_copy(h, cc, yy, zz, slot, sibling).wait_recv()
 
     def send_own(h):
-        for slot in (1, 3, 2, 7):
+        for slot in (2, 1, 3, 7):
             gather(h, slot).start()
 
     def relay_across(h):
         arrived(h, 0)
-        for slot in (4, 6, 5, 8):
+        for slot in (5, 4, 6, 8):
             gather(h, slot).start()
 
     def forward_own_row(h):
@@ -311,13 +311,13 @@
 
         @pl.when((h >= 1) & (h < heads))
         def _():
-            for j in (0, 2, 1):
+            for j in (1, 0, 2):
                 stage_x(done, j).start()
 
         @pl.when(h == heads)
         def _():
             last_v().start()
-            for j in (0, 2, 1):
+            for j in (1, 0, 2):
                 last_x(j).start()
 
         @pl.when(h == 1)
@@ -385,7 +385,7 @@
             total = acc_a[yh] + recv_a[done, yh].astype(F32) + recv_c[done].astype(F32)
             tot_b[...] = total
             send_b[done] = total.astype(BF16)
-            for j in (0, 2, 1):
+            for j in (1, 0, 2):
                 stage_b(done, j).start()
 
         @pl.when(h == heads + 1)
@@ -424,7 +424,7 @@
             total = dv_acc[pl.ds(pl.multiple_of(yl * rows, rows), rows), :].reshape(4, 128, hd) + recv_v[...].astype(F32)
             tot_w[...] = total
             send_w[...] = total.astype(BF16)
-            for j in (0, 2, 1):
+            for j in (1, 0, 2):
                 last_w(j).start()
             for j in range(3):
                 last_x(j).wait_recv()

time: 65.7 us -> 65.7 us (level)
  no operation moved by 1% of the time
where the time goes in v8:
time: 65.7 us; the launch traced here: 65.5 us
  Pallas kernels  64.2 us (98%)
  between operations  1.29 us (2%)
    pallas_call x1, Pallas kernels, shards(): pl.pallas_call(functools.partial(core, heads, tile), out_shape=jax.ShapeD...  62.4 us
    pallas_call x1, Pallas kernels, shards(): pl.pallas_call(finish, out_shape=(narrow, narrow, narrow), in_specs=[vmem...  1.75 us

profile of v8, /device:TPU:0, one launch (start us, length us, event | category | flops | bytes accessed | tf_op | source)
XLA Modules:
  0.0 65.5 jit_solution(8164305821396613867)
XLA Ops:
  1.3 62.4 %attention.1.sums_ref = bf16[3,128,512]{2,1,0:T(8,128)(2,1)} custom-call(s32[1,1]{1,0:T(1,128)S(6)} %copy.12.count_ref, s32[1,1,2,96]{3,2,1,0:T(2,128)} %list_ref.1, s32[1,1,96,8,128]{4,3,2,1,0:T(8,128)} %words_hbm.1, bf16[128,512]{1,0:T(8,128)(2,1)} %q_hbm.1, bf16[128,512]{1,0:T(8,128)(2,1)} %g_hbm.1, bf16[128,512]{1,0:T(8,128)(2,1)} %o_hbm.1, ...), custom_call_target="tpu_custom_call" | custom-call | tf_op jit(solution)/shard_map/attention/pallas_call | solution.py:565
  63.7 1.7 %finish.1 = (bf16[128,512]{1,0:T(8,128)(2,1)}, bf16[128,512]{1,0:T(8,128)(2,1)}, bf16[128,512]{1,0:T(8,128)(2,1)}) custom-call(bf16[3,128,512]{2,1,0:T(8,128)(2,1)} %attention.1.sums_ref), custom_call_target="tpu_custom_call" | custom-call | tf_op jit(solution)/shard_map/finish/pallas_call | solution.py:615
